TPU v7x, 32 devices: a whole 2x2x4 slice. The times are simulated.
32 devices in a mesh: dp: 8 (over y, x, core), mp: 4 (over z).
Axes of the slice: x: 2, y: 2, z: 4, core: 2. Of those that a mesh axis runs over, the one named last changes fastest.
Arguments:
- tokens_in: bfloat16 [16384, 640], P(('dp', 'mp')), may hold values from -6 to 6
- cotangent: bfloat16 [16384, 640], P(('dp', 'mp')), may hold values from -6 to 6
- lengths: int32 [8, 32], P('dp'), may hold values from 0 to 1024, as said below
- segments: int32 [8, 2048], P('dp'), may hold values from 0 to 32, as said below
- bucket_map: int32 [8], P('dp'), may hold values from 0 to 3, as said below
- bucket_tokens: int32 [4], replicated, may hold values from 256 to 65535
- attention: float32 [2, 4, 640, 640], P(None, None, 'dp', 'mp')
- feedforward: float32 [2, 2, 640, 5120], P(None, None, 'dp', 'mp')
- vectors: float32 [2, 6, 640], P(None, None, 'dp')
- head_bias: float32 [2, 2, 640], P(None, None, 'mp'), may hold values from -3 to 3
- unit_bias: float32 [2, 5120], P(None, 'mp'), may hold values from -3 to 3
- attention_moment: float32 [2, 4, 640, 640], P(None, None, 'dp', 'mp'), may hold values from -384 to 384
- feedforward_moment: float32 [2, 2, 640, 5120], P(None, None, 'dp', 'mp'), may hold values from -384 to 384
- vectors_moment: float32 [2, 6, 640], P(None, None, 'dp'), may hold values from -384 to 384
- head_moment: float32 [2, 2, 640], P(None, None, 'mp'), may hold values from -384 to 384
- unit_moment: float32 [2, 5120], P(None, 'mp'), may hold values from -384 to 384
- attention_mean: float32 [2, 4, 640, 640], P(None, None, 'dp', 'mp')
- feedforward_mean: float32 [2, 2, 640, 5120], P(None, None, 'dp', 'mp')
- vectors_mean: float32 [2, 6, 640], P(None, None, 'dp')
- head_mean: float32 [2, 2, 640], P(None, None, 'mp'), may hold values from -3 to 3
- unit_mean: float32 [2, 5120], P(None, 'mp'), may hold values from -3 to 3
Outputs:
- hidden_out: float32 [16384, 640], P(('dp', 'mp'))
- input_gradient: float32 [16384, 640], P(('dp', 'mp'))
- attention_gradient: float32 [2, 4, 640, 640], P(None, None, 'dp', 'mp')
- feedforward_gradient: float32 [2, 2, 640, 5120], P(None, None, 'dp', 'mp')
- vectors_gradient: float32 [2, 6, 640], P(None, None, 'dp')
- head_gradient: float32 [2, 2, 640], P(None, None, 'mp')
- unit_gradient: float32 [2, 5120], P(None, 'mp')
- attention_next: float32 [2, 4, 640, 640], P(None, None, 'dp', 'mp')
- feedforward_next: float32 [2, 2, 640, 5120], P(None, None, 'dp', 'mp')
- vectors_next: float32 [2, 6, 640], P(None, None, 'dp')
- head_next: float32 [2, 2, 640], P(None, None, 'mp')
- unit_next: float32 [2, 5120], P(None, 'mp')
- attention_momentum: float32 [2, 4, 640, 640], P(None, None, 'dp', 'mp')
- feedforward_momentum: float32 [2, 2, 640, 5120], P(None, None, 'dp', 'mp')
- vectors_momentum: float32 [2, 6, 640], P(None, None, 'dp')
- head_momentum: float32 [2, 2, 640], P(None, None, 'mp')
- unit_momentum: float32 [2, 5120], P(None, 'mp')
- attention_average: float32 [2, 4, 640, 640], P(None, None, 'dp', 'mp')
- feedforward_average: float32 [2, 2, 640, 5120], P(None, None, 'dp', 'mp')
- vectors_average: float32 [2, 6, 640], P(None, None, 'dp')
- head_average: float32 [2, 2, 640], P(None, None, 'mp')
- unit_average: float32 [2, 5120], P(None, 'mp')
- attention_copy: bfloat16 [2, 4, 640, 640], P(None, None, 'dp', 'mp')
- feedforward_copy: bfloat16 [2, 2, 640, 5120], P(None, None, 'dp', 'mp')
Inputs may be any that keep to these rules, and one draw needn't show every extreme that they name: In each pack the nonzero lengths stand first and are 20 or more; a pack's lengths sum to less than 2048; some pack holds a sequence of 1024. segments[p, t] is the number of sequences of pack p that end at or before position t, so positions past the sum of the pack's lengths hold 32. `bucket_map`: each bucket owns a run of 2 consecutive packs.
All inputs are finite; a program needn't handle non-finite values.
Results may differ from a plain program's by a relative error of at most 0.012.
Values may be sent and summed in bfloat16 or wider, within the bound.
A program may use at most 256 MiB of HBM per device.

v0:
```python
import math

import jax
import jax.numpy as jnp
from jax import lax
from jax.sharding import PartitionSpec as P

HEAD_DIM = 32


EPSILON = 1e-05
MOMENTUM = 0.9
AVERAGE_KEEP = 0.9
WEIGHT_DECAY = 0.0001
RATE_SCALE = 0.02
MASKED = -1e30
BLOCK_ROWS = 512


def layer_norm(hidden, gain_row, shift_row):
    centre = hidden - jnp.mean(hidden, axis=-1, keepdims=True)
    inverse = lax.rsqrt(jnp.mean(centre * centre, axis=-1, keepdims=True) + EPSILON)
    normal = centre * inverse
    return (normal * gain_row + shift_row, normal, inverse)


def norm_backward(upstream, normal, inverse, gain_row):
    scaled = upstream * gain_row
    result = inverse * (
        scaled
        - jnp.mean(scaled, axis=-1, keepdims=True)
        - normal * jnp.mean(scaled * normal, axis=-1, keepdims=True)
    )
    return (result, jnp.sum(upstream * normal, axis=0), jnp.sum(upstream, axis=0))


def gelu_slope(before):
    return 0.5 * (1.0 + lax.erf(before * (1.0 / math.sqrt(2.0)))) + before * jnp.exp(
        -0.5 * before * before
    ) * (1.0 / math.sqrt(2.0 * math.pi))


def gather_rows(local_rows):
    return lax.all_gather(local_rows, "mp", axis=0, tiled=True)


def gather_back(local_rows):
    return lax.all_gather(local_rows, "mp", axis=0, tiled=True)


def sum_forward(product_fn, row_count):
    return lax.psum_scatter(
        product_fn(jnp.int32(0), row_count * lax.axis_size("mp")),
        "mp",
        scatter_dimension=0,
        tiled=True,
    )


def sum_backward(product_fn, row_count):
    return lax.psum_scatter(
        product_fn(jnp.int32(0), row_count * lax.axis_size("mp")),
        "mp",
        scatter_dimension=0,
        tiled=True,
    )


def block_mask(segment_row, live_keys, first_row, block_size):
    positions = jnp.arange(segment_row.shape[0])
    query_place = first_row + jnp.arange(block_size)
    query_segment = lax.dynamic_slice_in_dim(segment_row, first_row, block_size, 0)
    return (query_segment[:, None] == segment_row[None, :]) & (
        live_keys[None, :] | (query_place[:, None] == positions[None, :])
    )


def attend_forward(queries, keys_all, values, segment_row, live_keys, block_size):
    pack_length = queries.shape[0]
    score_scale = HEAD_DIM ** (-0.5)
    block_starts = jnp.arange(pack_length // block_size, dtype=jnp.int32) * block_size

    def one_block(first_row):
        query_block = lax.dynamic_slice_in_dim(queries, first_row, block_size, 0)
        scores = (
            jnp.einsum("qhd,khd->hqk", query_block, keys_all, preferred_element_type=jnp.float32)
            * score_scale
        )
        scores = jnp.where(
            block_mask(segment_row, live_keys, first_row, block_size)[None], scores, MASKED
        )
        largest = jnp.max(scores, axis=-1, keepdims=True)
        exponent = jnp.exp(scores - largest)
        totals = jnp.sum(exponent, axis=-1, keepdims=True)
        probability = (exponent / totals).astype(jnp.bfloat16)
        mixed_rows = jnp.einsum(
            "hqk,khd->qhd", probability, values, preferred_element_type=jnp.float32
        )
        return (mixed_rows.astype(jnp.bfloat16), (largest + jnp.log(totals))[..., 0])

    mixed_rows, log_total = lax.map(one_block, block_starts)
    return (mixed_rows.reshape(pack_length, -1), log_total)


def attend_backward(
    queries, keys_all, values, upstream, log_total, segment_row, live_keys, block_size
):
    pack_length = queries.shape[0]
    score_scale = HEAD_DIM ** (-0.5)
    block_starts = jnp.arange(pack_length // block_size, dtype=jnp.int32) * block_size

    def one_block(carried, operands):
        key_sum, value_sum = carried
        first_row, block_total = operands
        query_block = lax.dynamic_slice_in_dim(queries, first_row, block_size, 0)
        grad_block = lax.dynamic_slice_in_dim(upstream, first_row, block_size, 0)
        scores = (
            jnp.einsum("qhd,khd->hqk", query_block, keys_all, preferred_element_type=jnp.float32)
            * score_scale
        )
        scores = jnp.where(
            block_mask(segment_row, live_keys, first_row, block_size)[None], scores, MASKED
        )
        probability = jnp.exp(scores - block_total[..., None])
        rounded = probability.astype(jnp.bfloat16)
        value_sum = value_sum + jnp.einsum(
            "hqk,qhd->khd", rounded, grad_block, preferred_element_type=jnp.float32
        )
        weight_slope = jnp.einsum(
            "qhd,khd->hqk", grad_block, values, preferred_element_type=jnp.float32
        )
        inner_sum = jnp.sum(probability * weight_slope, axis=-1, keepdims=True)
        score_grad = (probability * (weight_slope - inner_sum)).astype(jnp.bfloat16)
        query_grad = (
            jnp.einsum("hqk,khd->qhd", score_grad, keys_all, preferred_element_type=jnp.float32)
            * score_scale
        )
        key_sum = key_sum + jnp.einsum(
            "hqk,qhd->khd", score_grad, query_block, preferred_element_type=jnp.float32
        )
        return ((key_sum, value_sum), query_grad)

    empty_sum = jnp.zeros(queries.shape, jnp.float32)
    (key_sum, value_sum), query_grads = lax.scan(
        one_block, (empty_sum, empty_sum), (block_starts, log_total)
    )
    return (query_grads.reshape(queries.shape), key_sum * score_scale, value_sum)


def sgd_step(weight, gradient, moment, average, step_rate):
    decayed = gradient + WEIGHT_DECAY * weight
    moment_next = MOMENTUM * moment + decayed
    weight_next = weight - step_rate * (decayed + MOMENTUM * moment_next)
    average_next = AVERAGE_KEEP * average + (1.0 - AVERAGE_KEEP) * weight_next
    return (weight_next, moment_next, average_next)


def contract_rows(left, right):
    return lax.dot_general(
        left, right, (((0,), (0,)), ((), ())), preferred_element_type=jnp.float32
    )


def contract_last(left, right):
    return lax.dot_general(
        left, right, (((1,), (1,)), ((), ())), preferred_element_type=jnp.float32
    )


def local(
    tokens_in,
    cotangent,
    lengths,
    segments,
    bucket_map,
    bucket_tokens,
    attention,
    feedforward,
    vectors,
    head_bias,
    unit_bias,
    attention_moment,
    feedforward_moment,
    vectors_moment,
    head_moment,
    unit_moment,
    attention_mean,
    feedforward_mean,
    vectors_mean,
    head_mean,
    unit_mean,
):
    row_count = tokens_in.shape[0]
    model_parts = lax.axis_size("mp")
    pack_length = row_count * model_parts
    block_size = min(BLOCK_ROWS, pack_length)
    head_local = attention.shape[3] // HEAD_DIM
    layer_count = attention.shape[0]
    segment_row = segments[0]
    total_live = jnp.sum(lengths[0])
    live_keys = jnp.arange(pack_length) < total_live
    own_place = lax.axis_index("mp") * row_count + jnp.arange(row_count)
    live_own = (own_place < total_live)[:, None]
    counts_float = bucket_tokens.astype(jnp.float32)
    chosen = jnp.arange(bucket_tokens.shape[0]) == bucket_map[0]
    pack_weight = (
        bucket_tokens.shape[0]
        * jnp.sum(jnp.where(chosen, counts_float, 0.0))
        / jnp.sum(counts_float)
    )
    low_attention = attention.astype(jnp.bfloat16)
    low_feedforward = feedforward.astype(jnp.bfloat16)
    low_vectors = vectors.astype(jnp.bfloat16)
    full_attention, full_feedforward, full_vectors = (
        lax.all_gather(low_attention, "dp", axis=2, tiled=True),
        lax.all_gather(low_feedforward, "dp", axis=2, tiled=True),
        lax.all_gather(low_vectors, "dp", axis=2, tiled=True),
    )
    head_used = lax.optimization_barrier(head_bias.astype(jnp.bfloat16)).astype(jnp.float32)
    unit_used = lax.optimization_barrier(unit_bias.astype(jnp.bfloat16)).astype(jnp.float32)
    hidden = tokens_in.astype(jnp.float32)
    saved_layers = []
    for layer_index in range(layer_count):
        vector_rows = full_vectors[layer_index].astype(jnp.float32)
        normed_own, normal_one, inverse_one = layer_norm(hidden, vector_rows[0], vector_rows[1])
        normed = gather_rows(normed_own.astype(jnp.bfloat16))
        projected = jnp.einsum(
            "td,sde->ste",
            normed,
            full_attention[layer_index, :3],
            preferred_element_type=jnp.float32,
        )
        queries = (
            (projected[0] + head_used[layer_index, 0])
            .astype(jnp.bfloat16)
            .reshape(pack_length, head_local, HEAD_DIM)
        )
        keys_all = projected[1].astype(jnp.bfloat16).reshape(pack_length, head_local, HEAD_DIM)
        values = (
            (projected[2] + head_used[layer_index, 1])
            .astype(jnp.bfloat16)
            .reshape(pack_length, head_local, HEAD_DIM)
        )
        mixed_rows, log_total = attend_forward(
            queries, keys_all, values, segment_row, live_keys, block_size
        )
        out_weight = full_attention[layer_index, 3]

        def attention_rows(first_row, span_rows, mixed_rows=mixed_rows, out_weight=out_weight):
            return contract_last(mixed_rows, out_weight)

        hidden = hidden + (sum_forward(attention_rows, row_count) + vector_rows[4])
        normed_two_own, normal_two, inverse_two = layer_norm(hidden, vector_rows[2], vector_rows[3])
        normed_two = gather_rows(normed_two_own.astype(jnp.bfloat16))
        before = (
            jnp.dot(
                normed_two, full_feedforward[layer_index, 0], preferred_element_type=jnp.float32
            )
            + unit_used[layer_index]
        )
        activated = jax.nn.gelu(before, approximate=False).astype(jnp.bfloat16)
        down_weight = full_feedforward[layer_index, 1]

        def unit_rows(first_row, span_rows, activated=activated, down_weight=down_weight):
            return contract_last(activated, down_weight)

        hidden = hidden + (sum_forward(unit_rows, row_count) + vector_rows[5])
        saved_layers.append(
            (
                normed,
                normal_one,
                inverse_one,
                queries,
                keys_all,
                values,
                mixed_rows,
                log_total,
                normed_two,
                normal_two,
                inverse_two,
                before,
                activated,
            )
        )
    hidden_out = jnp.where(live_own, hidden, 0.0)
    back_attention, back_feedforward, back_vectors = (
        lax.all_gather(low_attention, "dp", axis=2, tiled=True),
        lax.all_gather(low_feedforward, "dp", axis=2, tiled=True),
        lax.all_gather(low_vectors, "dp", axis=2, tiled=True),
    )
    upstream = jnp.where(live_own, cotangent.astype(jnp.float32) * pack_weight, 0.0)
    attention_parts, feedforward_parts, vector_parts, head_parts, unit_parts = ([], [], [], [], [])
    for layer_index in reversed(range(layer_count)):
        (
            normed,
            normal_one,
            inverse_one,
            queries,
            keys_all,
            values,
            mixed_rows,
            log_total,
            normed_two,
            normal_two,
            inverse_two,
            before,
            activated,
        ) = saved_layers[layer_index]
        vector_rows = back_vectors[layer_index].astype(jnp.float32)
        branch_low = upstream.astype(jnp.bfloat16)
        down_bias_grad = jnp.sum(branch_low.astype(jnp.float32), axis=0)
        branch_full = gather_back(branch_low)
        down_grad = contract_rows(branch_full, activated)
        unit_slope = jnp.dot(
            branch_full, back_feedforward[layer_index, 1], preferred_element_type=jnp.float32
        )
        before_grad = (unit_slope * gelu_slope(before)).astype(jnp.bfloat16)
        up_grad = contract_rows(normed_two, before_grad)
        unit_bias_grad = jnp.sum(before_grad.astype(jnp.float32), axis=0)
        up_weight = back_feedforward[layer_index, 0]

        def unit_back(first_row, span_rows, before_grad=before_grad, up_weight=up_weight):
            return contract_last(before_grad, up_weight)

        normed_two_grad = sum_backward(unit_back, row_count)
        residual_part, gain_two_grad, shift_two_grad = norm_backward(
            normed_two_grad, normal_two, inverse_two, vector_rows[2]
        )
        upstream = upstream + residual_part
        branch_low = upstream.astype(jnp.bfloat16)
        out_bias_grad = jnp.sum(branch_low.astype(jnp.float32), axis=0)
        branch_full = gather_back(branch_low)
        out_grad = contract_rows(branch_full, mixed_rows)
        mixed_grad = jnp.dot(
            branch_full, back_attention[layer_index, 3], preferred_element_type=jnp.float32
        ).astype(jnp.bfloat16)
        query_grad, key_grad, value_grad = attend_backward(
            queries,
            keys_all,
            values,
            mixed_grad.reshape(pack_length, head_local, HEAD_DIM),
            log_total,
            segment_row,
            live_keys,
            block_size,
        )
        stacked = (
            jnp.stack([query_grad, key_grad, value_grad])
            .astype(jnp.bfloat16)
            .reshape(3, pack_length, head_local * HEAD_DIM)
        )
        projection_grad = jnp.einsum(
            "td,ste->sde", normed, stacked, preferred_element_type=jnp.float32
        )
        stacked_float = stacked.astype(jnp.float32)
        head_bias_grad = jnp.stack(
            [jnp.sum(stacked_float[0], axis=0), jnp.sum(stacked_float[2], axis=0)]
        )
        qkv_weight = back_attention[layer_index, :3]

        def attention_back(first_row, span_rows, stacked=stacked, qkv_weight=qkv_weight):
            return jnp.einsum(
                "ste,sde->td", stacked, qkv_weight, preferred_element_type=jnp.float32
            )

        normed_grad = sum_backward(attention_back, row_count)
        residual_part, gain_one_grad, shift_one_grad = norm_backward(
            normed_grad, normal_one, inverse_one, vector_rows[0]
        )
        upstream = upstream + residual_part
        layer_attention = jnp.stack(
            [projection_grad[0], projection_grad[1], projection_grad[2], out_grad]
        )
        layer_feedforward = jnp.stack([up_grad, down_grad])
        layer_vectors = jnp.stack(
            [
                gain_one_grad,
                shift_one_grad,
                gain_two_grad,
                shift_two_grad,
                out_bias_grad,
                down_bias_grad,
            ]
        )
        head_parts.append(head_bias_grad)
        unit_parts.append(unit_bias_grad)
        attention_parts.append(layer_attention)
        feedforward_parts.append(layer_feedforward)
        vector_parts.append(layer_vectors)
    head_local_grad = jnp.stack(head_parts[::-1])
    unit_local_grad = jnp.stack(unit_parts[::-1])
    attention_local = jnp.stack(attention_parts[::-1])
    feedforward_local = jnp.stack(feedforward_parts[::-1])
    vector_local = jnp.stack(vector_parts[::-1])
    vector_total = lax.psum(vector_local, "mp")
    attention_gradient, feedforward_gradient, vectors_gradient = (
        lax.psum_scatter(attention_local, "dp", scatter_dimension=2, tiled=True),
        lax.psum_scatter(feedforward_local, "dp", scatter_dimension=2, tiled=True),
        lax.psum_scatter(vector_total, "dp", scatter_dimension=2, tiled=True),
    )
    head_gradient, unit_gradient = lax.psum((head_local_grad, unit_local_grad), "dp")
    step_rate = RATE_SCALE * lax.rsqrt(jnp.float32(lax.axis_size("dp") * pack_length))
    attention_next, attention_momentum, attention_average = sgd_step(
        attention, attention_gradient, attention_moment, attention_mean, step_rate
    )
    feedforward_next, feedforward_momentum, feedforward_average = sgd_step(
        feedforward, feedforward_gradient, feedforward_moment, feedforward_mean, step_rate
    )
    vectors_next, vectors_momentum, vectors_average = sgd_step(
        vectors, vectors_gradient, vectors_moment, vectors_mean, step_rate
    )
    head_next, head_momentum, head_average = sgd_step(
        head_bias, head_gradient, head_moment, head_mean, step_rate
    )
    unit_next, unit_momentum, unit_average = sgd_step(
        unit_bias, unit_gradient, unit_moment, unit_mean, step_rate
    )
    return (
        hidden_out,
        upstream,
        attention_gradient,
        feedforward_gradient,
        vectors_gradient,
        head_gradient,
        unit_gradient,
        attention_next,
        feedforward_next,
        vectors_next,
        head_next,
        unit_next,
        attention_momentum,
        feedforward_momentum,
        vectors_momentum,
        head_momentum,
        unit_momentum,
        attention_average,
        feedforward_average,
        vectors_average,
        head_average,
        unit_average,
        attention_next.astype(jnp.bfloat16),
        feedforward_next.astype(jnp.bfloat16),
    )


def solution(mesh):
    in_specs = (
        P(("dp", "mp"), None),
        P(("dp", "mp"), None),
        P("dp", None),
        P("dp", None),
        P("dp"),
        P(),
        P(None, None, "dp", "mp"),
        P(None, None, "dp", "mp"),
        P(None, None, "dp"),
        P(None, None, "mp"),
        P(None, "mp"),
        P(None, None, "dp", "mp"),
        P(None, None, "dp", "mp"),
        P(None, None, "dp"),
        P(None, None, "mp"),
        P(None, "mp"),
        P(None, None, "dp", "mp"),
        P(None, None, "dp", "mp"),
        P(None, None, "dp"),
        P(None, None, "mp"),
        P(None, "mp"),
    )
    out_specs = (
        P(("dp", "mp"), None),
        P(("dp", "mp"), None),
        P(None, None, "dp", "mp"),
        P(None, None, "dp", "mp"),
        P(None, None, "dp"),
        P(None, None, "mp"),
        P(None, "mp"),
        P(None, None, "dp", "mp"),
        P(None, None, "dp", "mp"),
        P(None, None, "dp"),
        P(None, None, "mp"),
        P(None, "mp"),
        P(None, None, "dp", "mp"),
        P(None, None, "dp", "mp"),
        P(None, None, "dp"),
        P(None, None, "mp"),
        P(None, "mp"),
        P(None, None, "dp", "mp"),
        P(None, None, "dp", "mp"),
        P(None, None, "dp"),
        P(None, None, "mp"),
        P(None, "mp"),
        P(None, None, "dp", "mp"),
        P(None, None, "dp", "mp"),
    )
    return jax.shard_map(local, mesh=mesh, in_specs=in_specs, out_specs=out_specs, check_vma=False)
```

profile of v0, /device:TPU:0, one launch (start us, length us, event | category | flops | bytes accessed | tf_op | source)
XLA Modules:
  0.0 2445.2 jit_solution(7015682285808679939)
XLA Ops:
  64.7 43.0 %all-gather.11.cloned.1.call-done = bf16[2048,640]{1,0:T(8,128)(2,1)} async-done(((bf16[512,640]{1,0:T(8,128)(2,1)}), bf16[2048,640]{1,0:T(8,128)(2,1)}) %all-gather.11.cloned.1.call-update) | async-done | bytes 2621456 | tf_op jit(solution)/shard_map/all_gather | solution.py:44
  113.6 135.1 %while.56 = (s32[]{:T(128)}, bf16[4,512,5,32]{1,3,2,0:T(8,128)(2,1)S(1)}, f32[4,5,512]{2,1,0:T(8,128)S(1)}, s32[4]{0:T(128)S(1)}, s32[2048]{0:T(1024)S(1)}, /*in...) while((s32[]{:T(128)}, ...), condition=%wide.region_6.7_spmd.clone, body=%wide.region_3.6_spmd.clone.sunk | while | flops 738279424 | bytes 152768752 | solution.py:101
  256.8 90.1 %reduce-scatter.16.cloned.1.call-done = f32[512,640]{1,0:T(8,128)} async-done(((f32[2048,640]{1,0:T(8,128)}), f32[512,640]{1,0:T(8,128)}) %reduce-scatter.16.cloned.1.call-update) | async-done | bytes 1310736 | tf_op jit(solution)/shard_map/reduce_scatter | solution.py:52
  350.7 45.6 %all-gather.17.cloned.1.call-done = bf16[2,2,640,1280]{3,2,1,0:T(8,128)(2,1)} async-done(((bf16[2,2,80,1280]{3,2,1,0:T(8,128)(2,1)}), bf16[2,2,640,1280]{3,2,1,0:T(8,128)(2,1)}) %all-gather.17.cloned.1.call-update) | async-done | bytes 6553616 | tf_op jit(solution)/shard_map/all_gather | solution.py:216
  396.3 56.8 %all-gather.15.cloned.1.call-done = bf16[2048,640]{1,0:T(8,128)(2,1)} async-done(((bf16[512,640]{1,0:T(8,128)(2,1)}), bf16[2048,640]{1,0:T(8,128)(2,1)}) %all-gather.15.cloned.1.call-update) | async-done | bytes 2621456 | tf_op jit(solution)/shard_map/all_gather | solution.py:44
  453.1 28.0 %fusion.90 = (bf16[2048,1280]{1,0:T(8,128)(2,1)S(1)}, f32[2048,1280]{1,0:T(8,128)}) fusion(f32[1280]{0:T(1024)S(1)} %get-tuple-element.567, bf16[2048,640]{1,0:T(8,128)(2,1)} %all-gather.15.cloned.1.call-done, bf16[2,2,640,1280]{3,2,1,0:T(8,128)(2,1)} %all-gather.17.cloned.1.call-done), kind=kOutput, calls=%fused_computation.113 | convolution fusion | flops 3528458240 | bytes 19993600 | tf_op jit(solution)/shard_map/dot_general | solution.py:256
  491.0 92.6 %reduce-scatter.18.cloned.1.call-done = f32[512,640]{1,0:T(8,128)} async-done(((f32[2048,640]{1,0:T(8,128)}), f32[512,640]{1,0:T(8,128)}) %reduce-scatter.18.cloned.1.call-update) | async-done | bytes 1310736 | tf_op jit(solution)/shard_map/reduce_scatter | solution.py:52
  590.5 52.4 %all-gather.19.cloned.1.call-done = bf16[2048,640]{1,0:T(8,128)(2,1)} async-done(((bf16[512,640]{1,0:T(8,128)(2,1)}), bf16[2048,640]{1,0:T(8,128)(2,1)}) %all-gather.19.cloned.1.call-update) | async-done | bytes 2621456 | tf_op jit(solution)/shard_map/all_gather | solution.py:44
  648.8 134.9 %while.57 = (s32[]{:T(128)}, bf16[4,512,5,32]{1,3,2,0:T(8,128)(2,1)S(1)}, f32[4,5,512]{2,1,0:T(8,128)S(1)}, s32[4]{0:T(128)S(1)}, s32[2048]{0:T(1024)S(1)}, /*in...) while((s32[]{:T(128)}, ...), condition=%wide.region_16.17_spmd.clone, body=%wide.region_13.16_spmd.clone.sunk | while | flops 738279424 | bytes 152768752 | solution.py:101
  788.7 92.6 %reduce-scatter.20.cloned.1.call-done = f32[512,640]{1,0:T(8,128)} async-done(((f32[2048,640]{1,0:T(8,128)}), f32[512,640]{1,0:T(8,128)}) %reduce-scatter.20.cloned.1.call-update) | async-done | bytes 1310736 | tf_op jit(solution)/shard_map/reduce_scatter | solution.py:52
  890.1 50.4 %all-gather.21.cloned.1.call-done = bf16[2048,640]{1,0:T(8,128)(2,1)} async-done(((bf16[512,640]{1,0:T(8,128)(2,1)}), bf16[2048,640]{1,0:T(8,128)(2,1)}) %all-gather.21.cloned.1.call-update) | async-done | bytes 2621456 | tf_op jit(solution)/shard_map/all_gather | solution.py:44
  940.5 28.5 %fusion.93 = (bf16[2048,1280]{1,0:T(8,128)(2,1)}, f32[2048,1280]{1,0:T(8,128)}) fusion(f32[1280]{0:T(1024)S(1)} %copy-done.104, bf16[2048,640]{1,0:T(8,128)(2,1)} %all-gather.21.cloned.1.call-done, bf16[2,2,640,1280]{3,2,1,0:T(8,128)(2,1)} %all-gather.17.cloned.1.call-done), kind=kOutput, calls=%fused_computation.116 | convolution fusion | flops 3528458240 | bytes 19993600 | tf_op jit(solution)/shard_map/dot_general | solution.py:256
  1026.4 82.5 %reduce-scatter.24.cloned.1.call-done = f32[512,640]{1,0:T(8,128)} async-done(((f32[2048,640]{1,0:T(8,128)}), f32[512,640]{1,0:T(8,128)}) %reduce-scatter.24.cloned.1.call-update) | async-done | bytes 1310736 | tf_op jit(solution)/shard_map/reduce_scatter | solution.py:61
  1111.5 93.9 %reduce-scatter.22.cloned.1.call-done = f32[512,640]{1,0:T(8,128)} async-done(((f32[2048,640]{1,0:T(8,128)}), f32[512,640]{1,0:T(8,128)}) %reduce-scatter.22.cloned.1.call-update) | async-done | bytes 1310736 | tf_op jit(solution)/shard_map/reduce_scatter | solution.py:52
  1209.5 55.3 %all-gather.25.cloned.1.call-done = bf16[2048,640]{1,0:T(8,128)(2,1)} async-done(((bf16[512,640]{1,0:T(8,128)(2,1)}), bf16[2048,640]{1,0:T(8,128)(2,1)}) %all-gather.25.cloned.1.call-update) | async-done | bytes 2621456 | tf_op jit(solution)/shard_map/all_gather | solution.py:48
  1269.4 252.1 %while.58 = (s32[]{:T(128)}, f32[2048,5,32]{0,2,1:T(8,128)}, f32[2048,5,32]{0,2,1:T(8,128)}, bf16[4,512,5,32]{1,3,2,0:T(8,128)(2,1)}, s32[4]{0:T(128)S(1)}, /*in...) while((s32[]{:T(128)}, f32[2048,5,32]{0,2,1:T(8,128)}, ...), condition=%wide.region_28.29_spmd.clone, body=%wide.region_26.28_spmd.clone.sunk | while | flops 1761951744 | bytes 264139056 | solution.py:144
  1531.3 92.6 %reduce-scatter.26.cloned.1.call-done = f32[512,640]{1,0:T(8,128)} async-done(((f32[2048,640]{1,0:T(8,128)}), f32[512,640]{1,0:T(8,128)}) %reduce-scatter.26.cloned.1.call-update) | async-done | bytes 1310736 | tf_op jit(solution)/shard_map/reduce_scatter | solution.py:61
  1630.2 55.3 %all-gather.27.cloned.1.call-done = bf16[2048,640]{1,0:T(8,128)(2,1)} async-done(((bf16[512,640]{1,0:T(8,128)(2,1)}), bf16[2048,640]{1,0:T(8,128)(2,1)}) %all-gather.27.cloned.1.call-update) | async-done | bytes 2621456 | tf_op jit(solution)/shard_map/all_gather | solution.py:48
  1705.8 92.7 %reduce-scatter.28.cloned.1.call-done = f32[512,640]{1,0:T(8,128)} async-done(((f32[2048,640]{1,0:T(8,128)}), f32[512,640]{1,0:T(8,128)}) %reduce-scatter.28.cloned.1.call-update) | async-done | bytes 1310736 | tf_op jit(solution)/shard_map/reduce_scatter | solution.py:61
  1812.2 48.0 %all-gather.29.cloned.1.call-done = bf16[2048,640]{1,0:T(8,128)(2,1)} async-done(((bf16[512,640]{1,0:T(8,128)(2,1)}), bf16[2048,640]{1,0:T(8,128)(2,1)}) %all-gather.29.cloned.1.call-update) | async-done | bytes 2621456 | tf_op jit(solution)/shard_map/all_gather | solution.py:48
  1864.7 254.8 %while.59 = (s32[]{:T(128)}, f32[2048,5,32]{0,2,1:T(8,128)}, f32[2048,5,32]{0,2,1:T(8,128)}, bf16[4,512,5,32]{1,3,2,0:T(8,128)(2,1)}, s32[4]{0:T(128)S(1)}, /*in...) while((s32[]{:T(128)}, f32[2048,5,32]{0,2,1:T(8,128)}, ...), condition=%wide.region_37.38_spmd.clone, body=%wide.region_35.37_spmd.clone.sunk | while | flops 1761951744 | bytes 264139056 | solution.py:144
  2238.1 50.6 %reduce-scatter.32.cloned.1.call-done = f32[2,2,80,1280]{3,2,1,0:T(8,128)} async-done(((f32[2,2,640,1280]{3,2,1,0:T(8,128)}), f32[2,2,80,1280]{3,2,1,0:T(8,128)}) %reduce-scatter.32.cloned.1.call-update) | async-done | bytes 1638416 | tf_op jit(solution)/shard_map/reduce_scatter | solution.py:398
  2294.1 90.5 %reduce-scatter.30.cloned.1.call-done = f32[512,640]{1,0:T(8,128)} async-done(((f32[2048,640]{1,0:T(8,128)}), f32[512,640]{1,0:T(8,128)}) %reduce-scatter.30.cloned.1.call-update) | async-done | bytes 1310736 | tf_op jit(solution)/shard_map/reduce_scatter | solution.py:61
  2391.4 31.2 %reduce-scatter.36.cloned.1.call-done = f32[80,12]{1,0:T(8,128)} async-done(((f32[640,12]{1,0:T(8,128)}), f32[80,12]{1,0:T(8,128)}) %reduce-scatter.36.cloned.1.call-update) | async-done | bytes 3856
  (695 shorter events, 1120.2 us)
Async XLA Ops:
  7.2 46.8 %all-gather.13.cloned.1.call-start = ((), (), s32[]{:S(2)}) async-start(), calls=%async_computation.12 | async-start | bytes 2949120 | tf_op jit(solution)/shard_map/all_gather | solution.py:215
  9.6 98.1 %all-gather.11.cloned.1.call-start = ((), (), s32[]{:S(2)}) async-start(), calls=%async_computation.11 | async-start | bytes 3276800 | tf_op jit(solution)/shard_map/all_gather | solution.py:44
  52.5 294.4 %reduce-scatter.16.cloned.1.call-start = ((), (), s32[]{:S(2)}) async-start(), calls=%async_computation.13 | async-start | bytes 6553600 | tf_op jit(solution)/shard_map/reduce_scatter | solution.py:52
  254.2 142.1 %all-gather.17.cloned.1.call-start = ((), (), s32[]{:S(2)}) async-start(), calls=%async_computation.15 | async-start | bytes 7372800 | tf_op jit(solution)/shard_map/all_gather | solution.py:216
  256.8 196.3 %all-gather.15.cloned.1.call-start = ((), (), s32[]{:S(2)}) async-start(), calls=%async_computation.14 | async-start | bytes 3276800 | tf_op jit(solution)/shard_map/all_gather | solution.py:44
  348.5 235.1 %copy-start.10 = (f32[512,640]{1,0:T(8,128)}, f32[512,640]{1,0:T(8,128)S(1)}, u32[]{:S(2)}) copy-start(f32[512,640]{1,0:T(8,128)S(1)} %get-tuple-element.697) | copy-start | bytes 3932164
  350.0 233.6 %reduce-scatter.18.cloned.1.call-start = ((), (), s32[]{:S(2)}) async-start(), calls=%async_computation.16 | async-start | bytes 6553600 | tf_op jit(solution)/shard_map/reduce_scatter | solution.py:52
  490.9 151.9 %all-gather.19.cloned.1.call-start = ((), (), s32[]{:S(2)}) async-start(), calls=%async_computation.17 | async-start | bytes 3276800 | tf_op jit(solution)/shard_map/all_gather | solution.py:44
  587.5 293.9 %reduce-scatter.20.cloned.1.call-start = ((), (), s32[]{:S(2)}) async-start(), calls=%async_computation.18 | async-start | bytes 6553600 | tf_op jit(solution)/shard_map/reduce_scatter | solution.py:52
  788.6 151.8 %all-gather.21.cloned.1.call-start = ((), (), s32[]{:S(2)}) async-start(), calls=%async_computation.19 | async-start | bytes 3276800 | tf_op jit(solution)/shard_map/all_gather | solution.py:44
  885.1 110.9 %all-gather.23.cloned.1.call-start = ((), (), s32[]{:S(2)}) async-start(), calls=%async_computation.21 | async-start | bytes 3276800 | tf_op jit(solution)/shard_map/all_gather | solution.py:48
  890.1 218.8 %reduce-scatter.24.cloned.1.call-start = ((), (), s32[]{:S(2)}) async-start(), calls=%async_computation.22 | async-start | bytes 6553600 | tf_op jit(solution)/shard_map/reduce_scatter | solution.py:61
  1016.2 189.2 %reduce-scatter.22.cloned.1.call-start = ((), (), s32[]{:S(2)}) async-start(), calls=%async_computation.20 | async-start | bytes 6553600 | tf_op jit(solution)/shard_map/reduce_scatter | solution.py:52
  1026.3 179.1 %copy-start.90 = (f32[640]{0:T(1024)S(1)}, f32[640]{0:T(1024)}, u32[]{:S(2)}) copy-start(f32[640]{0:T(1024)} %get-tuple-element.554) | copy-start | bytes 7684
  1026.4 238.5 %all-gather.25.cloned.1.call-start = ((), (), s32[]{:S(2)}) async-start(), calls=%async_computation.23 | async-start | bytes 3276800 | tf_op jit(solution)/shard_map/all_gather | solution.py:48
  1209.5 414.4 %reduce-scatter.26.cloned.1.call-start = ((), (), s32[]{:S(2)}) async-start(), calls=%async_computation.24 | async-start | bytes 6553600 | tf_op jit(solution)/shard_map/reduce_scatter | solution.py:61
  1531.2 154.3 %copy-start.103 = (f32[1280]{0:T(1024)S(1)}, f32[1280]{0:T(1024)}, u32[]{:S(2)}) copy-start(f32[1280]{0:T(1024)} %copy-done.102) | copy-start | bytes 15364
  1531.2 154.3 %all-gather.27.cloned.1.call-start = ((), (), s32[]{:S(2)}) async-start(), calls=%async_computation.25 | async-start | bytes 3276800 | tf_op jit(solution)/shard_map/all_gather | solution.py:48
  1630.2 168.3 %reduce-scatter.28.cloned.1.call-start = ((), (), s32[]{:S(2)}) async-start(), calls=%async_computation.26 | async-start | bytes 6553600 | tf_op jit(solution)/shard_map/reduce_scatter | solution.py:61
  1705.8 154.5 %all-gather.29.cloned.1.call-start = ((), (), s32[]{:S(2)}) async-start(), calls=%async_computation.27 | async-start | bytes 3276800 | tf_op jit(solution)/shard_map/all_gather | solution.py:48
  1804.8 419.5 %reduce-scatter.34.cloned.1.call-start = ((), (), s32[]{:S(2)}) async-start(), calls=%async_computation.30 | async-start | bytes 3686400
  2144.1 144.6 %reduce-scatter.32.cloned.1.call-start = ((), (), s32[]{:S(2)}) async-start(), calls=%async_computation.29 | async-start | bytes 14745600 | tf_op jit(solution)/shard_map/reduce_scatter | solution.py:398
  2183.2 201.4 %reduce-scatter.30.cloned.1.call-start = ((), (), s32[]{:S(2)}) async-start(), calls=%async_computation.28 | async-start | bytes 6553600 | tf_op jit(solution)/shard_map/reduce_scatter | solution.py:61
  2189.0 233.6 %reduce-scatter.36.cloned.1.call-start = ((), (), s32[]{:S(2)}) async-start(), calls=%async_computation.31 | async-start | bytes 368640
  (149 other events, 5003.4 us)
Sparse Core Ops, SparseCore 0:
  10.5 32.6 all-gather.12
  52.6 55.0 all-gather.10
  254.3 92.5 reduce-scatter.15
  349.2 46.9 all-gather.16
  398.3 54.7 all-gather.14
  491.0 92.5 reduce-scatter.17
  587.6 55.2 all-gather.18
  788.7 92.5 reduce-scatter.19
  885.2 55.2 all-gather.20
  942.5 53.5 all-gather.22
  1016.3 92.5 reduce-scatter.23
  1111.1 94.2 reduce-scatter.21
  1209.6 55.2 all-gather.24
  1531.3 92.5 reduce-scatter.25
  1630.3 55.2 all-gather.26
  1705.9 92.5 reduce-scatter.27
  1804.9 55.3 all-gather.28
  2144.2 45.4 reduce-scatter.33
  2193.9 94.7 reduce-scatter.31
  2290.8 93.7 reduce-scatter.29
  2388.3 34.3 reduce-scatter.35
where the time goes:
time: 2460 us; the launch traced here: 2450 us
  waiting for transfers between devices  1240 us (50%)
  matrix products  567 us (23%)
  other arithmetic  298 us (12%)
  local copies, waits for them, and re-layouts  235 us (10%)
  blocking collectives  46.9 us (2%)
  loops' own time  33.9 us (1%)
    reduce_scatter x4, waiting for transfers between devices, sum_forward(): lax.psum_scatter(product_fn(jnp.int32(0), row_count * lax.axis_size('mp')...  369 us
    reduce_scatter x4, waiting for transfers between devices, sum_backward(): lax.psum_scatter(product_fn(jnp.int32(0), row_count * lax.axis_size('mp')...  358 us
    all_gather x4, waiting for transfers between devices, gather_rows(): return lax.all_gather(local_rows, 'mp', axis=0, tiled=True)  203 us
    all_gather x4, waiting for transfers between devices, gather_back(): return lax.all_gather(local_rows, 'mp', axis=0, tiled=True)  186 us
    dot_general x8, matrix products, one_block(): jnp.einsum('qhd,khd->hqk', grad_block, values, preferred_element_type=jnp...  124 us
    while x64, local copies, waits for them, and re-layouts  120 us
    convert_element_type x8, other arithmetic, one_block(): score_grad = (probability * (weight_slope - inner_sum)).astype(jnp.bfloat16)  118 us
    dot_general x8, matrix products, one_block(): jnp.einsum('hqk,khd->qhd', probability, values, preferred_element_type=jn...  79.8 us
  transfers between devices with their start and end apart: 21, of which 19 were waited for; matrix products, arithmetic and copies ran while one was open for 7% of the time, Pallas kernels for 0%

commit v1 on v0

v1 whole, which is shorter than its diff:
```python
import functools, math
import jax, jax.numpy as jnp
from jax import lax
from jax.experimental import pallas as pl
from jax.experimental.pallas import tpu as pltpu
from jax.sharding import PartitionSpec as P

HEAD_DIM = 32
MASKED = -1e30
LOG2E = math.log2(math.e)
SCORE = HEAD_DIM ** (-0.5)
SCORE2 = SCORE * LOG2E
BLK = 256
BF = jnp.bfloat16
F32 = jnp.float32
VMEM_LIMIT = 60 * 1024 * 1024


def cost(micros):
    return pl.CostEstimate(flops=micros * 1100000000, bytes_accessed=1000000, transcendentals=0)


def dot_nn(a, b):
    return lax.dot_general(a, b, (((1,), (0,)), ((), ())), preferred_element_type=F32)


def dot_nt(a, b):
    return lax.dot_general(a, b, (((1,), (1,)), ((), ())), preferred_element_type=F32)


def load_parts(scal, parts, dest, first, rows, sem, axis):
    copies = []
    for i, part in enumerate(parts):
        start = pl.multiple_of(scal[first + i] * rows, rows)
        at = dest.at[pl.ds(start, rows)] if axis == 0 else dest.at[:, pl.ds(start, rows)]
        copies.append(pltpu.make_async_copy(part, at, sem))
    for copy in copies:
        copy.start()
    return copies


def attn_fwd_kernel(nb, npc, *refs):
    scal = refs[0]
    xparts = refs[1:5]
    wparts = refs[5:5 + npc]
    bias, segk, segq, out, lse = refs[5 + npc:10 + npc]
    xs, ws, ks, qt, vt, acc, scores, sems = refs[10 + npc:]
    heads = ks.shape[0]
    width = heads * HEAD_DIM
    rows = xparts[0].shape[0]
    base = 2 * nb
    wcopies = load_parts(scal, wparts, ws, base + 5, wparts[0].shape[0], sems.at[4], 0)
    xcopies = [load_parts(scal, [p], xs, base + i, rows, sems.at[i], 0)[0] for i, p in enumerate(xparts)]
    for c in wcopies:
        c.wait()
    for i in range(4):
        xcopies[i].wait()
        start = pl.multiple_of(scal[base + i] * rows, rows)
        y = dot_nn(xs[pl.ds(start, rows), :], ws[...])
        qt[:, pl.ds(start, rows)] = (y[:, :width] + bias[0:1, :]).T.astype(BF)
        k = y[:, width:2 * width].astype(BF)
        for h in range(heads):
            ks[h, pl.ds(start, rows), :] = k[:, h * HEAD_DIM:(h + 1) * HEAD_DIM]
        vt[:, pl.ds(start, rows)] = (y[:, 2 * width:] + bias[1:2, :]).T.astype(BF)
    lse[...] = jnp.zeros_like(lse)
    per = rows // BLK

    def fold(z):
        return z.reshape(BLK // 8, 8, BLK)

    def q_block(qb, carry):
        q0 = pl.multiple_of(qb * BLK, BLK)
        acc[...] = jnp.zeros_like(acc)
        sq = segq[:, pl.ds(q0, BLK)]
        first, end = scal[qb], scal[nb + qb]

        def score_block(kb, ms):
            k0 = pl.multiple_of(kb * BLK, BLK)
            mask = segk[pl.ds(k0, BLK), :] == sq
            new = []
            for h in range(heads):
                hs = slice(h * HEAD_DIM, (h + 1) * HEAD_DIM)
                s = dot_nn(ks[h, pl.ds(k0, BLK), :], qt[hs, pl.ds(q0, BLK)])
                s = jnp.where(mask, s, MASKED)
                scores[h, kb] = s
                new.append(jnp.maximum(ms[h], jnp.max(fold(s), axis=0)))
            return tuple(new)

        ms = lax.fori_loop(first, end, score_block, (jnp.full((8, BLK), MASKED, F32),) * heads)
        tops = [jnp.max(m, axis=0, keepdims=True) * SCORE2 for m in ms]

        def mix_block(kb, ls):
            k0 = pl.multiple_of(kb * BLK, BLK)
            new = []
            for h in range(heads):
                hs = slice(h * HEAD_DIM, (h + 1) * HEAD_DIM)
                p = jnp.exp2(scores[h, kb] * SCORE2 - tops[h])
                acc[hs, :] += dot_nn(vt[hs, pl.ds(k0, BLK)], p.astype(BF))
                new.append(ls[h] + jnp.sum(fold(p), axis=0))
            return tuple(new)

        ls = lax.fori_loop(first, end, mix_block, (jnp.zeros((8, BLK), F32),) * heads)
        for h in range(heads):
            hs = slice(h * HEAD_DIM, (h + 1) * HEAD_DIM)
            l = jnp.sum(ls[h], axis=0, keepdims=True)
            acc[hs, :] = acc[hs, :] * (1.0 / l)
            lse[h:h + 1, pl.ds(q0, BLK)] = tops[h] + jnp.log2(l)
        part = lax.bitwise_xor(lax.div(qb, per), scal[base])
        out[part, pl.ds(pl.multiple_of(lax.rem(qb, per) * BLK, BLK), BLK), :] = acc[...].T.astype(BF)
        return carry

    lax.fori_loop(0, nb, q_block, 0)


def attn_fwd(scal, xparts, wparts, bias, segk, segq):
    rows, d = xparts[0].shape
    t = 4 * rows
    width = wparts[0].shape[1] // 3
    heads = width // HEAD_DIM
    nb = t // BLK
    npc = len(wparts)
    anyspec = pl.BlockSpec(memory_space=pl.ANY)
    v = pl.BlockSpec(memory_space=pltpu.VMEM)
    return pl.pallas_call(
        functools.partial(attn_fwd_kernel, nb, npc),
        out_shape=(jax.ShapeDtypeStruct((4, rows, width), BF), jax.ShapeDtypeStruct((8, t), F32)),
        in_specs=[pl.BlockSpec(memory_space=pltpu.SMEM)] + [anyspec] * (4 + npc) + [v] * 3,
        out_specs=(v, v),
        scratch_shapes=[
            pltpu.VMEM((t, d), BF), pltpu.VMEM((d, 3 * width), BF), pltpu.VMEM((heads, t, HEAD_DIM), BF),
            pltpu.VMEM((width, t), BF), pltpu.VMEM((width, t), BF), pltpu.VMEM((width, BLK), F32),
            pltpu.VMEM((heads, nb, BLK, BLK), F32),
            pltpu.SemaphoreType.DMA((5,)),
        ],
        compiler_params=pltpu.CompilerParams(vmem_limit_bytes=VMEM_LIMIT),
        cost_estimate=cost(28),
        name="attention_forward",
    )(scal, *xparts, *wparts, bias, segk, segq)


def attn_bwd_kernel(nb, npc, groups, *refs):
    scal = refs[0]
    xparts = refs[1:5]
    wparts = refs[5:5 + npc]
    daparts = refs[5 + npc:9 + npc]
    a_saved, bias, segk, segq, lse, dx, dbias = refs[9 + npc:16 + npc]
    dw_out = refs[16 + npc:16 + npc + groups]
    xs, ws, qs, ks, vs, das, qt, kt, dat, delta, dqt, dall, dka, dva, dw, sems, osem = refs[16 + npc + groups:]
    heads = ks.shape[0]
    width = heads * HEAD_DIM
    rows = xparts[0].shape[0]
    base = 2 * nb
    wcopies = load_parts(scal, wparts, ws, base + 5, wparts[0].shape[0], sems.at[4], 0)
    xcopies = [load_parts(scal, [p], xs, base + i, rows, sems.at[i], 0)[0] for i, p in enumerate(xparts)]
    for c in wcopies:
        c.wait()
    for i in range(4):
        xcopies[i].wait()
        start = pl.multiple_of(scal[base + i] * rows, rows)
        at = pl.ds(start, rows)
        x = xs[at, :]
        y = dot_nn(x, ws[...])
        q = y[:, :width] + bias[0:1, :]
        qt[:, at] = q.T.astype(BF)
        ql = q.astype(BF)
        kf = y[:, width:2 * width]
        kt[:, at] = kf.T.astype(BF)
        kl = kf.astype(BF)
        vl = (y[:, 2 * width:] + bias[1:2, :]).astype(BF)
        dal = daparts[i][...]
        daf = dal.astype(F32).T
        dat[:, at] = daf.astype(BF)
        prod = daf * a_saved[i].astype(F32).T
        for h in range(heads):
            hs = slice(h * HEAD_DIM, (h + 1) * HEAD_DIM)
            qs[h, at, :] = ql[:, hs]
            ks[h, at, :] = kl[:, hs]
            vs[h, at, :] = vl[:, hs]
            das[h, at, :] = dal[:, hs]
            delta[h:h + 1, at] = jnp.sum(prod[hs, :], axis=0, keepdims=True)
    dqt[...] = jnp.zeros_like(dqt)

    def k_block(kb, carry):
        k0 = pl.multiple_of(kb * BLK, BLK)
        kat = pl.ds(k0, BLK)
        dka[...] = jnp.zeros_like(dka)
        dva[...] = jnp.zeros_like(dva)
        sk = segk[kat, :]

        def q_block(qb, c2):
            q0 = pl.multiple_of(qb * BLK, BLK)
            qat = pl.ds(q0, BLK)
            mask = sk == segq[:, qat]
            for h in range(heads):
                hs = slice(h * HEAD_DIM, (h + 1) * HEAD_DIM)
                s = dot_nn(ks[h, kat, :], qt[hs, qat])
                p = jnp.where(mask, jnp.exp2(s * SCORE2 - lse[h:h + 1, qat]), 0.0)
                dp = dot_nn(vs[h, kat, :], dat[hs, qat])
                dva[h] += dot_nn(p.astype(BF), das[h, qat, :])
                ds = (p * (dp - delta[h:h + 1, qat])).astype(BF)
                dka[h] += dot_nn(ds, qs[h, qat, :])
                dqt[hs, qat] += dot_nn(kt[hs, kat], ds)
            return c2

        lax.fori_loop(scal[kb], scal[nb + kb], q_block, 0)
        for h in range(heads):
            hs = slice(h * HEAD_DIM, (h + 1) * HEAD_DIM)
            dall[width + h * HEAD_DIM:width + (h + 1) * HEAD_DIM, kat] = (dka[h].T * SCORE).astype(BF)
            dall[2 * width + h * HEAD_DIM:2 * width + (h + 1) * HEAD_DIM, kat] = dva[h].T.astype(BF)
        return carry

    lax.fori_loop(0, nb, k_block, 0)
    dall[:width, :] = (dqt[...] * SCORE).astype(BF)
    dbias[0:1, :] = jnp.sum(dall[:width, :].astype(F32), axis=1)[None, :]
    dbias[1:2, :] = jnp.sum(dall[2 * width:, :].astype(F32), axis=1)[None, :]
    dw[...] = dot_nn(dall[...], xs[...]).T.astype(dw.dtype)
    rows_d, per = wparts[0].shape[0], npc // groups
    stores = []
    for p in range(npc):
        at = pl.ds(pl.multiple_of(scal[base + 5 + p] * rows_d, rows_d), rows_d)
        stores.append(pltpu.make_async_copy(dw.at[at], dw_out[p // per].at[p % per], osem))
        stores[-1].start()
    for i in range(4):
        start = pl.multiple_of(scal[base + i] * rows, rows)
        at = pl.ds(start, rows)
        dx[i] = dot_nt(dall[:, at].astype(F32).T.astype(BF), ws[...]).astype(BF)
    for copy in stores:
        copy.wait()


def attn_bwd(scal, xparts, wparts, daparts, a_saved, bias, segk, segq, lse, groups):
    rows, d = xparts[0].shape
    t = 4 * rows
    width = wparts[0].shape[1] // 3
    heads = width // HEAD_DIM
    nb = t // BLK
    npc = len(wparts)
    anyspec = pl.BlockSpec(memory_space=pl.ANY)
    v = pl.BlockSpec(memory_space=pltpu.VMEM)
    head_rows = pltpu.VMEM((heads, t, HEAD_DIM), BF)
    flat = pltpu.VMEM((width, t), BF)
    return pl.pallas_call(
        functools.partial(attn_bwd_kernel, nb, npc, groups),
        out_shape=(
            jax.ShapeDtypeStruct((4, rows, d), BF),
            jax.ShapeDtypeStruct((2, width), F32),
        ) + (jax.ShapeDtypeStruct((npc // groups, wparts[0].shape[0], 3 * width), BF),) * groups,
        in_specs=[pl.BlockSpec(memory_space=pltpu.SMEM)] + [anyspec] * (4 + npc) + [v] * 9,
        out_specs=(v, v) + (anyspec,) * groups,
        scratch_shapes=[
            pltpu.VMEM((t, d), BF), pltpu.VMEM((d, 3 * width), BF),
            head_rows, head_rows, head_rows, head_rows, flat, flat, flat,
            pltpu.VMEM((8, t), F32), pltpu.VMEM((width, t), F32), pltpu.VMEM((3 * width, t), BF),
            pltpu.VMEM((heads, BLK, HEAD_DIM), F32), pltpu.VMEM((heads, BLK, HEAD_DIM), F32),
            pltpu.VMEM((d, 3 * width), BF), pltpu.SemaphoreType.DMA((5,)), pltpu.SemaphoreType.DMA(()),
        ],
        compiler_params=pltpu.CompilerParams(vmem_limit_bytes=VMEM_LIMIT),
        cost_estimate=cost(55),
        name="attention_backward",
    )(scal, *xparts, *wparts, *daparts, a_saved, bias, segk, segq, lse)


EPSILON = 1e-05
SUB = 640


def normal_rows(hidden):
    centre = hidden - jnp.mean(hidden, axis=-1, keepdims=True)
    inverse = lax.rsqrt(jnp.mean(centre * centre, axis=-1, keepdims=True) + EPSILON)
    return centre * inverse, inverse


def norm_back(upstream, normal, inverse, gain_row):
    scaled = upstream * gain_row
    return inverse * (scaled - jnp.mean(scaled, axis=-1, keepdims=True) - normal * jnp.mean(scaled * normal, axis=-1, keepdims=True))


def gelu_share(u):
    return 0.5 * (1.0 + lax.erf(u * (1.0 / math.sqrt(2.0))))


def start_weights(scal, first, wo_parts, w1_parts, w2_parts, wo, w1, w2, sems):
    def spans(parts):
        rows = parts[0].shape[1]
        return [pl.ds(pl.multiple_of(scal[first + i] * rows, rows), rows) for i in range(len(parts))]
    by_block = [[] for _ in range(5)]
    for part, at in zip(wo_parts, spans(wo_parts)):
        by_block[0].append(pltpu.make_async_copy(part, wo.at[:, at], sems.at[0]))
    for z in range(4):
        for dest, parts in ((w1, w1_parts), (w2, w2_parts)):
            for part, at in zip(parts, spans(parts)):
                by_block[1 + z].append(pltpu.make_async_copy(part.at[z], dest.at[z, at], sems.at[1 + z]))
    for copies in by_block:
        for copy in copies:
            copy.start()
    return by_block


def wait_all(copies):
    for copy in copies:
        copy.wait()


def post_fwd_kernel(npc, last, *refs):
    scal = refs[0]
    a, hidden, vec, ub = refs[1:5]
    wo_parts, w1_parts, w2_parts = refs[5:5 + npc], refs[5 + npc:5 + 2 * npc], refs[5 + 2 * npc:5 + 3 * npc]
    rest = refs[5 + 3 * npc:]
    outs, (wo, w1, w2, xn2, sems) = rest[:-5], rest[-5:]
    h1, h2 = outs[:2]
    loads = start_weights(scal, 1, wo_parts, w1_parts, w2_parts, wo, w1, w2, sems)
    wait_all(loads[0])
    total = hidden[...] + vec[4:5, :]
    for i in range(4):
        total += dot_nt(a[i], wo[lax.bitwise_xor(i, scal[0])])
    h1[...] = total
    normal, _ = normal_rows(total)
    xn2[...] = (normal * vec[2:3, :] + vec[3:4, :]).astype(BF)
    h2[...] = total + vec[5:6, :]
    units = w1.shape[2]
    for z in range(4):
        wait_all(loads[1 + z])

        def step(j, carry):
            at = pl.ds(pl.multiple_of(j * SUB, SUB), SUB)
            u = dot_nn(xn2[...], w1[z, :, at]) + ub[z, :, at]
            g = (u * gelu_share(u)).astype(BF)
            h2[...] += dot_nt(g, w2[z, :, at])
            return carry

        lax.fori_loop(0, units // SUB, step, 0)
    if not last:
        normal, _ = normal_rows(h2[...])
        outs[2][...] = (normal * vec[8:9, :] + vec[9:10, :]).astype(BF)


def post_fwd(scal, a, hidden, vec, ub, wo_parts, w1_parts, w2_parts, last):
    rows, d = hidden.shape
    npc = len(w1_parts)
    width, units = wo_parts[0].shape[2], w1_parts[0].shape[2]
    anyspec = pl.BlockSpec(memory_space=pl.ANY)
    v = pl.BlockSpec(memory_space=pltpu.VMEM)
    out = [jax.ShapeDtypeStruct((rows, d), F32)] * 2 + ([] if last else [jax.ShapeDtypeStruct((rows, d), BF)])
    return pl.pallas_call(
        functools.partial(post_fwd_kernel, npc, last),
        out_shape=out,
        in_specs=[pl.BlockSpec(memory_space=pltpu.SMEM)] + [v] * 4 + [anyspec] * (3 * npc),
        out_specs=[v] * len(out),
        scratch_shapes=[
            pltpu.VMEM((4, d, width), BF), pltpu.VMEM((4, d, units), BF), pltpu.VMEM((4, d, units), BF),
            pltpu.VMEM((rows, d), BF), pltpu.SemaphoreType.DMA((5,)),
        ],
        compiler_params=pltpu.CompilerParams(vmem_limit_bytes=VMEM_LIMIT),
        cost_estimate=cost(16),
        name="rows_forward",
    )(scal, a, hidden, vec, ub, *wo_parts, *w1_parts, *w2_parts)


def post_bwd_kernel(npc, groups, *refs):
    scal = refs[0]
    a, h1, gy, vec, ub = refs[1:6]
    wo_parts, w1_parts, w2_parts = refs[6:6 + npc], refs[6 + npc:6 + 2 * npc], refs[6 + 2 * npc:6 + 3 * npc]
    rest = refs[6 + 3 * npc:]
    gy1, da_out, dub, dvec = rest[:4]
    dwo_out, dw1_out, dw2_out = rest[4:4 + groups], rest[4 + groups:4 + 2 * groups], rest[4 + 2 * groups:4 + 3 * groups]
    wo, w1, w2, dwo, dw1, dw2, xn2, df, xn2t, dft, dxn2, sems, osem = rest[4 + 3 * groups:]
    loads = start_weights(scal, 1, wo_parts, w1_parts, w2_parts, wo, w1, w2, sems)
    per = npc // groups
    rows_d = w1_parts[0].shape[1]
    spans = [pl.ds(pl.multiple_of(scal[1 + i] * rows_d, rows_d), rows_d) for i in range(npc)]
    normal, inverse = normal_rows(h1[...])
    xlow = (normal * vec[2:3, :] + vec[3:4, :]).astype(BF)
    xn2[...] = xlow
    xn2t[...] = xlow.T
    low = gy[...].astype(BF)
    df[...] = low
    dft[...] = low.T
    dvec[...] = jnp.zeros_like(dvec)
    dvec[5:6, :] = jnp.sum(low.astype(F32), axis=0, keepdims=True)
    dxn2[...] = jnp.zeros_like(dxn2)
    units = w1.shape[2]
    stores = []
    for z in range(4):
        wait_all(loads[1 + z])

        def step(j, carry):
            at = pl.ds(pl.multiple_of(j * SUB, SUB), SUB)
            u = dot_nn(xn2[...], w1[z, :, at]) + ub[z, :, at]
            share = gelu_share(u)
            g = (u * share).astype(BF)
            dg = dot_nn(df[...], w2[z, :, at])
            slope = share + u * jnp.exp(-0.5 * u * u) * (1.0 / math.sqrt(2.0 * math.pi))
            du = (dg * slope).astype(BF)
            dub[z, :, at] = jnp.sum(du.astype(F32), axis=0, keepdims=True)
            dw1[z, :, at] = dot_nn(xn2t[...], du).astype(BF)
            dw2[z, :, at] = dot_nn(dft[...], g).astype(BF)
            dxn2[...] += dot_nt(du, w1[z, :, at])
            return carry

        lax.fori_loop(0, units // SUB, step, 0)
        for p in range(npc):
            for src, outs in ((dw1, dw1_out), (dw2, dw2_out)):
                stores.append(pltpu.make_async_copy(src.at[z, spans[p]], outs[p // per].at[p % per, z], osem))
                stores[-1].start()
    wait_all(loads[0])
    upstream = dxn2[...]
    dvec[2:3, :] = jnp.sum(upstream * normal, axis=0, keepdims=True)
    dvec[3:4, :] = jnp.sum(upstream, axis=0, keepdims=True)
    total = gy[...] + norm_back(upstream, normal, inverse, vec[2:3, :])
    gy1[...] = total
    low = total.astype(BF)
    dvec[4:5, :] = jnp.sum(low.astype(F32), axis=0, keepdims=True)
    dat = low.T
    for i in range(4):
        slot = lax.bitwise_xor(i, scal[0])
        dwo[slot] = dot_nn(dat, a[i]).astype(BF)
        da_out[i] = dot_nn(low, wo[slot]).astype(BF)
    for p in range(npc):
        stores.append(pltpu.make_async_copy(dwo.at[:, spans[p]], dwo_out[p // per].at[p % per], osem))
        stores[-1].start()
    wait_all(stores)


def post_bwd(scal, a, h1, gy, vec, ub, wo_parts, w1_parts, w2_parts, groups):
    rows, d = h1.shape
    npc = len(w1_parts)
    per = npc // groups
    rows_d, width, units = wo_parts[0].shape[1], wo_parts[0].shape[2], w1_parts[0].shape[2]
    anyspec = pl.BlockSpec(memory_space=pl.ANY)
    v = pl.BlockSpec(memory_space=pltpu.VMEM)
    out = [jax.ShapeDtypeStruct((rows, d), F32), jax.ShapeDtypeStruct((4, rows, width), BF),
           jax.ShapeDtypeStruct((4, 1, units), F32), jax.ShapeDtypeStruct((8, d), F32)]
    out += [jax.ShapeDtypeStruct((per, 4, rows_d, width), BF)] * groups
    out += [jax.ShapeDtypeStruct((per, 4, rows_d, units), BF)] * (2 * groups)
    return pl.pallas_call(
        functools.partial(post_bwd_kernel, npc, groups),
        out_shape=out,
        in_specs=[pl.BlockSpec(memory_space=pltpu.SMEM)] + [v] * 5 + [anyspec] * (3 * npc),
        out_specs=[v] * 4 + [anyspec] * (3 * groups),
        scratch_shapes=[
            pltpu.VMEM((4, d, width), BF), pltpu.VMEM((4, d, units), BF), pltpu.VMEM((4, d, units), BF),
            pltpu.VMEM((4, d, width), BF), pltpu.VMEM((4, d, units), BF), pltpu.VMEM((4, d, units), BF),
            pltpu.VMEM((rows, d), BF), pltpu.VMEM((rows, d), BF), pltpu.VMEM((d, rows), BF), pltpu.VMEM((d, rows), BF),
            pltpu.VMEM((rows, d), F32), pltpu.SemaphoreType.DMA((5,)), pltpu.SemaphoreType.DMA(()),
        ],
        compiler_params=pltpu.CompilerParams(vmem_limit_bytes=VMEM_LIMIT),
        cost_estimate=cost(33),
        name="rows_backward",
    )(scal, a, h1, gy, vec, ub, *wo_parts, *w1_parts, *w2_parts)


MOMENTUM = 0.9
AVERAGE_KEEP = 0.9
WEIGHT_DECAY = 0.0001
RATE_SCALE = 0.02
ROWS_AXES = ("y", "x", "c")
COLS_AXES = ("h", "b")
EVERY = ROWS_AXES + COLS_AXES


def swap(value, name):
    return lax.ppermute(value, name, [(0, 1), (1, 0)])


def home(value):
    return lax.ppermute(value, ("c", "h"), [(0, 0), (1, 2), (2, 1), (3, 3)])


def corner(value):
    return lax.ppermute(value, ("c", "b"), [(0, 3), (1, 2), (2, 1), (3, 0)])


def double(value, name):
    return jnp.concatenate([value, swap(value, name)], axis=0)


def plane_parts(value, x_first):
    across = swap(value, "x")
    along = swap(value, "y")
    both = swap(across, "y") if x_first else swap(along, "x")
    return [value, across, along, both]


def core_parts(parts):
    return parts + [swap(part, "c") for part in parts]


def f32(value):
    return value.astype(F32)


def reduce_plane(terms, x_first):
    def pick(dy, dx):
        return sum(f32(t[2 * dy + dx]) for t in terms)

    if x_first:
        got = swap(jnp.stack([pick(0, 1), pick(1, 1)]).astype(BF), "x")
        got2 = swap((pick(1, 0) + f32(got[1])).astype(BF), "y")
    else:
        got = swap(jnp.stack([pick(1, 0), pick(1, 1)]).astype(BF), "y")
        got2 = swap((pick(0, 1) + f32(got[1])).astype(BF), "x")
    return lambda index: pick(0, 0)[index] + f32(got[0][index]) + f32(got2[index])


def reduce_line(take):
    got = swap(take(slice(2, 4)).astype(BF), "h")
    got2 = swap((take(1) + f32(got[1])).astype(BF), "b")
    return take(0) + f32(got[0]) + f32(got2)


def sgd_step(weight, gradient, moment, average, step_rate):
    decayed = gradient + WEIGHT_DECAY * weight
    moment_next = MOMENTUM * moment + decayed
    weight_next = weight - step_rate * (decayed + MOMENTUM * moment_next)
    average_next = AVERAGE_KEEP * average + (1.0 - AVERAGE_KEEP) * weight_next
    return (weight_next, moment_next, average_next)


def local(
    tokens_in, cotangent, lengths, segments, bucket_map, bucket_tokens,
    attention, feedforward, vectors, head_bias, unit_bias,
    attention_moment, feedforward_moment, vectors_moment, head_moment, unit_moment,
    attention_mean, feedforward_mean, vectors_mean, head_mean, unit_mean,
):
    rows, width_d = tokens_in.shape
    layer_count = attention.shape[0]
    iy, ix, ic, ih, ib = (lax.axis_index(name) for name in EVERY)
    x_size = lax.axis_size("x")
    fast = lax.axis_size("y") == 2 and x_size == 2
    dp_size = lax.axis_size("y") * x_size * 2
    dp_place = (iy * x_size + ix) * 2 + ic
    mp_place = 2 * ih + ib
    quarter = 2 * ic + ib
    stays = ic == ih
    pack_length = rows * 4
    nb = pack_length // BLK

    low_attention, low_feedforward, low_vectors, low_head, low_unit = lax.optimization_barrier(
        tuple(p.astype(BF) for p in (attention, feedforward, vectors, head_bias, unit_bias))
    )

    hidden_low = home(tokens_in)
    meta = jnp.concatenate([segments[0], jnp.sum(lengths[0])[None], bucket_map])
    meta = jnp.where(stays, meta, swap(meta, "c"))
    segment_row, total_live, bucket = meta[:pack_length], meta[pack_length], meta[pack_length + 1]

    if fast:
        v8 = double(double(double(low_vectors.reshape(1, layer_count * 6, -1), "c"), "x"), "y")
        v8 = v8.reshape(2, 2, 2, layer_count * 6, -1)
        for axis, place in ((0, iy), (1, ix), (2, ic)):
            v8 = jnp.where(place == 1, jnp.flip(v8, axis), v8)
        full_vectors = v8.reshape(8, layer_count * 6, -1).transpose(1, 0, 2).reshape(layer_count, 6, width_d)
        units4 = double(double(low_unit[None], "b"), "h")
        heads_used = jnp.where(stays, low_head, swap(low_head, "h"))
        qkv_parts, wo_parts, up_parts, down_parts = [], [], [], []
        for layer in range(layer_count):
            qkv = jnp.concatenate([low_attention[layer, i] for i in range(3)], axis=1)
            far = swap(qkv, "h")
            mine = plane_parts(jnp.where(stays, qkv, far), True)
            theirs = plane_parts(jnp.where(stays, far, qkv), False)
            qkv_parts.append(mine + [swap(part, "c") for part in theirs])
            wo_parts.append(core_parts(plane_parts(double(double(low_attention[layer, 3][None], "b"), "h"), layer % 2 == 0)))
            up_parts.append(core_parts(plane_parts(double(double(low_feedforward[layer, 0][None], "b"), "h"), True)))
            down_parts.append(core_parts(plane_parts(double(double(low_feedforward[layer, 1][None], "b"), "h"), False)))
        chunk_places = [dp_place ^ (2 * (p % 4) + p // 4) for p in range(8)]
        switch = 2 * (ic ^ ih)
        groups = 2
    else:
        full_vectors = lax.all_gather(low_vectors, ROWS_AXES, axis=2, tiled=True)
        units4 = lax.all_gather(low_unit, COLS_AXES, axis=0)
        heads_used = lax.all_gather(low_head, COLS_AXES, axis=0)[quarter]
        whole_attention = lax.all_gather(lax.all_gather(low_attention, ROWS_AXES, axis=2, tiled=True), COLS_AXES, axis=0)
        whole_feedforward = lax.all_gather(lax.all_gather(low_feedforward, ROWS_AXES, axis=2, tiled=True), COLS_AXES, axis=0)
        own = whole_attention[quarter]
        qkv_parts = [[jnp.concatenate([own[layer, i] for i in range(3)], axis=1)] for layer in range(layer_count)]
        wo_parts = [[whole_attention[:, layer, 3]] for layer in range(layer_count)]
        up_parts = [[whole_feedforward[:, layer, 0]] for layer in range(layer_count)]
        down_parts = [[whole_feedforward[:, layer, 1]] for layer in range(layer_count)]
        chunk_places = [jnp.int32(0)]
        switch = quarter
        groups = 1
    vec = f32(full_vectors)
    unit_rows = f32(units4)
    head_rows = f32(heads_used)

    positions = jnp.arange(pack_length, dtype=jnp.int32)
    own_segment = jnp.where(positions < total_live, segment_row, 64 + positions)
    by_block = own_segment.reshape(nb, BLK)
    first_block = jnp.sum(own_segment[None, :] < by_block[:, :1], axis=1) // BLK
    end_block = (jnp.sum(own_segment[None, :] <= by_block[:, -1:], axis=1) + BLK - 1) // BLK
    places = jnp.stack([quarter ^ rel for rel in range(4)])
    chunk_array = jnp.stack(chunk_places).astype(jnp.int32)
    scal = jnp.concatenate([first_block, end_block, places, jnp.zeros((1,), jnp.int32), chunk_array]).astype(jnp.int32)
    scal_rows = jnp.concatenate([jnp.reshape(switch, (1,)).astype(jnp.int32), chunk_array])
    segk, segq = own_segment[:, None], own_segment[None, :]
    live_own = (quarter * rows + jnp.arange(rows) < total_live)[:, None]
    counts_float = f32(bucket_tokens)
    chosen = jnp.arange(bucket_tokens.shape[0]) == bucket
    pack_weight = bucket_tokens.shape[0] * jnp.sum(jnp.where(chosen, counts_float, 0.0)) / jnp.sum(counts_float)

    def vec_rows(layer, other):
        return jnp.concatenate([vec[layer], jnp.zeros((2, width_d), F32), vec[other], jnp.zeros((2, width_d), F32)])

    hidden = f32(hidden_low)
    normal, _ = normal_rows(hidden)
    normed = (normal * vec[0, 0] + vec[0, 1]).astype(BF)
    saved = []
    for layer in range(layer_count):
        last = layer == layer_count - 1
        over = swap(normed, "b")
        normed_parts = [normed, over, swap(normed, "c"), swap(over, "c")]
        mixed, log_total = attn_fwd(scal, normed_parts, qkv_parts[layer], head_rows[layer], segk, segq)
        own_mixed = jnp.stack([mixed[0], swap(mixed[1], "b"), swap(mixed[2], "c"), corner(mixed[3])])
        unit_row = unit_rows[:, layer][:, None, :]
        vec16 = vec_rows(layer, 0 if last else layer + 1)
        outs = post_fwd(scal_rows, own_mixed, hidden, vec16, unit_row, wo_parts[layer], up_parts[layer], down_parts[layer], last)
        saved.append((hidden, normed_parts, mixed, log_total, own_mixed, outs[0], unit_row, vec16))
        hidden = outs[1]
        if not last:
            normed = outs[2]
    hidden_out = home(jnp.where(live_own, hidden, 0.0))

    upstream = jnp.where(live_own, f32(home(cotangent)) * pack_weight, 0.0)
    attention_grads, feedforward_grads, vector_grads, head_grads, unit_grads = [], [], [], [], []
    for layer in reversed(range(layer_count)):
        hidden, normed_parts, mixed, log_total, own_mixed, middle, unit_row, vec16 = saved[layer]
        outs = post_bwd(scal_rows, own_mixed, middle, upstream, vec16, unit_row, wo_parts[layer], up_parts[layer], down_parts[layer], groups)
        upstream, d_mixed, d_unit, d_vec = outs[:4]
        d_wo, d_up, d_down = outs[4:4 + groups], outs[4 + groups:4 + 2 * groups], outs[4 + 2 * groups:4 + 3 * groups]
        d_parts = [d_mixed[0], swap(d_mixed[1], "b"), swap(d_mixed[2], "c"), corner(d_mixed[3])]
        outs = attn_bwd(scal, normed_parts, qkv_parts[layer], d_parts, mixed, head_rows[layer], segk, segq, log_total, groups)
        d_rows, d_head = outs[:2]
        d_qkv = outs[2:]
        got = swap(d_rows[2:4], "c")
        got2 = swap((f32(d_rows[1]) + f32(got[1])).astype(BF), "b")
        d_normed = f32(d_rows[0]) + f32(got[0]) + f32(got2)
        normal, inverse = normal_rows(hidden)
        upstream = upstream + norm_back(d_normed, normal, inverse, vec[layer, 0])
        vector_grads.append(jnp.concatenate([
            jnp.sum(d_normed * normal, axis=0)[None], jnp.sum(d_normed, axis=0)[None], d_vec[2:6]]))
        head_grads.append(d_head)
        unit_grads.append(d_unit[:, 0])
        if fast:
            up_grad, down_grad, wo_grad = (
                reduce_line(reduce_plane([keep, swap(send, "c")], x_first))
                for (keep, send), x_first in ((d_up, False), (d_down, True), (d_wo, layer % 2 == 0))
            )
            other = swap(d_qkv[1], "c")
            near = jnp.where(stays, d_qkv[0], other)
            far = jnp.where(stays, other, d_qkv[0])
            take = reduce_plane([jnp.stack([near, far], axis=1)], layer % 2 == 0)
            qkv_grad = take(0) + f32(swap(take(1).astype(BF), "h"))
        else:
            def scatter(value):
                value = lax.psum_scatter(f32(value), COLS_AXES, scatter_dimension=0, tiled=True)[0]
                return lax.psum_scatter(value, ROWS_AXES, scatter_dimension=0, tiled=True)

            up_grad, down_grad, wo_grad = scatter(d_up[0][0]), scatter(d_down[0][0]), scatter(d_wo[0][0])
            empty = jnp.zeros((4,) + d_qkv[0].shape[1:], F32)
            qkv_grad = scatter(empty.at[quarter].set(f32(d_qkv[0][0])))
        head_width = attention.shape[3]
        attention_grads.append(jnp.stack([qkv_grad[:, i * head_width:(i + 1) * head_width] for i in range(3)] + [wo_grad]))
        feedforward_grads.append(jnp.stack([up_grad, down_grad]))
    attention_gradient = jnp.stack(attention_grads[::-1])
    feedforward_gradient = jnp.stack(feedforward_grads[::-1])

    vector_sum = jnp.stack(vector_grads[::-1])
    head_sum = jnp.stack(head_grads[::-1])
    unit_sum = jnp.stack(unit_grads[::-1], axis=1)
    v_size, u_size, e_size = vector_sum.size, unit_sum.size // 4, head_sum.size
    if fast:
        flat_v, flat_e = vector_sum.reshape(-1), head_sum.reshape(-1)
        flat_u = unit_sum.reshape(4, -1)
        near = jnp.where(stays, flat_e, 0.0)
        got = swap(jnp.concatenate([flat_v, flat_u[2], flat_u[3], flat_e - near]), "h")
        flat_v = flat_v + got[:v_size]
        flat_e = near + got[v_size + 2 * u_size:]
        near_u = flat_u[0] + got[v_size:v_size + u_size]
        got2 = swap(jnp.concatenate([flat_v, flat_u[1] + got[v_size + u_size:v_size + 2 * u_size]]), "b")
        flat = jnp.concatenate([flat_v + got2[:v_size], near_u + got2[v_size:], flat_e])
        for name in ROWS_AXES:
            flat = flat + swap(flat, name)
        vector_total = flat[:v_size].reshape(vector_sum.shape)
        unit_gradient = flat[v_size:v_size + u_size].reshape(unit_bias.shape)
        head_gradient = flat[v_size + u_size:].reshape(head_bias.shape)
    else:
        placed = jnp.zeros((4,) + head_sum.shape, F32).at[quarter].set(head_sum)
        vector_total, unit_total, head_total = lax.psum((vector_sum, unit_sum, placed), EVERY)
        unit_gradient, head_gradient = unit_total[mp_place], head_total[mp_place]
    chunk = width_d // dp_size
    vectors_gradient = lax.dynamic_slice_in_dim(vector_total, dp_place * chunk, chunk, 2)

    input_gradient = f32(home(upstream.astype(BF)))
    input_gradient = jnp.where(stays, upstream, input_gradient)
    step_rate = RATE_SCALE * lax.rsqrt(jnp.float32(dp_size * pack_length))
    weights = (attention, feedforward, vectors, head_bias, unit_bias)
    gradients = (attention_gradient, feedforward_gradient, vectors_gradient, head_gradient, unit_gradient)
    moments = (attention_moment, feedforward_moment, vectors_moment, head_moment, unit_moment)
    averages = (attention_mean, feedforward_mean, vectors_mean, head_mean, unit_mean)
    steps = [sgd_step(*leaf, step_rate) for leaf in zip(weights, gradients, moments, averages)]
    return (
        (hidden_out, input_gradient) + gradients + tuple(s[0] for s in steps) + tuple(s[1] for s in steps)
        + tuple(s[2] for s in steps) + (steps[0][0].astype(BF), steps[1][0].astype(BF))
    )


def solution(mesh):
    dp_size = mesh.shape["dp"]
    inner = jax.sharding.Mesh(mesh.devices.reshape(2, dp_size // 4, 2, 2, 2), EVERY)
    rows, cols = ROWS_AXES, COLS_AXES
    tokens = P(rows + cols, None)
    params = (P(None, None, rows, cols), P(None, None, rows, cols), P(None, None, rows), P(None, None, cols), P(None, cols))
    in_specs = (tokens, tokens, P(rows, None), P(rows, None), P(rows), P()) + params * 3
    out_specs = (tokens, tokens) + params * 4 + params[:2]
    return jax.shard_map(local, mesh=inner, in_specs=in_specs, out_specs=out_specs, check_vma=False)
```

time: 2460 us -> 904 us (0.37)
  waiting for transfers between devices: 1240 us -> 395 us
  matrix products: 567 us -> 0 us
  Pallas kernels: 0 us -> 244 us
  other arithmetic: 298 us -> 68.2 us
  local copies, waits for them, and re-layouts: 235 us -> 36.5 us
  starting transfers between devices: 1.51 us -> 153 us
  blocking collectives: 46.9 us -> 0 us
  loops' own time: 33.9 us -> 0 us
    reduce_scatter x9 -> x0, waiting for transfers between devices: 778 us -> none  [the longest x4 369 us: sum_forward(): lax.psum_scatter(product_fn(jnp.int32(0), row_count * lax.axis_size('mp')...]
    dot_general x78 -> x0, matrix products: 561 us -> none  [the longest x8 124 us: one_block(): jnp.einsum('qhd,khd->hqk', grad_block, values, preferred_element_type=jnp...]
    all_gather x10 -> x0, waiting for transfers between devices: 434 us -> none  [the longest x4 203 us: gather_rows(): return lax.all_gather(local_rows, 'mp', axis=0, tiled=True)]
    ppermute x0 -> x152, waiting for transfers between devices: none -> 395 us  [the longest x144 381 us: swap(): return lax.ppermute(value, name, [(0, 1), (1, 0)])]
    pallas_call x0 -> x8, Pallas kernels: none -> 244 us  [the longest x2 96.2 us: attn_bwd(): pl.pallas_call(functools.partial(attn_bwd_kernel, nb, npc, groups), out_s...]
    ppermute x0 -> x152, starting transfers between devices: none -> 153 us  [the longest x144 135 us: swap(): return lax.ppermute(value, name, [(0, 1), (1, 0)])]
    while x66 -> x0, local copies, waits for them, and re-layouts: 121 us -> none
    convert_element_type x27 -> x38, other arithmetic: 140 us -> 25.3 us  [the longest x4 5.75 us: reduce_plane(): got2 = swap((pick(1, 0) + f32(got[1])).astype(BF), 'y')]
  transfers between devices with their start and end apart: 21 -> 152, of which waited for: 19 -> 60; matrix products, arithmetic and copies ran while one was open for 7% -> 9% of each run, Pallas kernels for 0% -> 23%
where the time goes in v1:
time: 904 us; the launch traced here: 902 us
  waiting for transfers between devices  395 us (44%)
  Pallas kernels  244 us (27%)
  starting transfers between devices  153 us (17%)
  other arithmetic  68.2 us (8%)
  local copies, waits for them, and re-layouts  36.5 us (4%)
    ppermute x144, waiting for transfers between devices, swap(): return lax.ppermute(value, name, [(0, 1), (1, 0)])  381 us
    ppermute x144, starting transfers between devices, swap(): return lax.ppermute(value, name, [(0, 1), (1, 0)])  135 us
    pallas_call x2, Pallas kernels, attn_bwd(): pl.pallas_call(functools.partial(attn_bwd_kernel, nb, npc, groups), out_s...  96.2 us
    pallas_call x2, Pallas kernels, post_bwd(): pl.pallas_call(functools.partial(post_bwd_kernel, npc, groups), out_shape...  67.1 us
    pallas_call x2, Pallas kernels, attn_fwd(): pl.pallas_call(functools.partial(attn_fwd_kernel, nb, npc), out_shape=(ja...  47.2 us
    pallas_call x2, Pallas kernels, post_fwd(): pl.pallas_call(functools.partial(post_fwd_kernel, npc, last), out_shape=o...  33.3 us
  transfers between devices with their start and end apart: 152, of which 60 were waited for; matrix products, arithmetic and copies ran while one was open for 9% of the time, Pallas kernels for 23%

profile of v1, /device:TPU:0, one launch (start us, length us, event | category | flops | bytes accessed | tf_op | source)
XLA Modules:
  0.0 901.7 jit_solution(9804372471365647150)
XLA Ops:
  16.9 12.5 %collective-permute-done.19 = bf16[2,2,160]{2,1,0:T(2,128)(2,1)S(1)} collective-permute-done((bf16[2,2,160]{2,1,0:T(2,128)(2,1)S(1)}, bf16[2,2,160]{2,1,0:T(2,128)(2,1)S(1)}, u32[]{:S(2)}, u32[]{:S(2)}) %collective-permute-start.19) | collective-permute-done | bytes 1312 | tf_op jit(solution)/shard_map/ppermute | solution.py:462
  100.1 19.9 %collective-permute-done.35 = bf16[2,80,1280]{2,1,0:T(8,128)(2,1)S(1)} collective-permute-done((bf16[2,80,1280]{2,1,0:T(8,128)(2,1)S(1)}, bf16[2,80,1280]{2,1,0:T(8,128)(2,1)S(1)}, u32[]{:S(2)}, u32[]{:S(2)}) %collective-permute-start.35) | collective-permute-done | bytes 409632 | tf_op jit(solution)/shard_map/ppermute | solution.py:462
  120.8 16.7 %collective-permute-done.44 = bf16[2,80,1280]{2,1,0:T(8,128)(2,1)S(1)} collective-permute-done((bf16[2,80,1280]{2,1,0:T(8,128)(2,1)S(1)}, bf16[2,80,1280]{2,1,0:T(8,128)(2,1)S(1)}, u32[]{:S(2)}, u32[]{:S(2)}) %collective-permute-start.44) | collective-permute-done | bytes 409632 | tf_op jit(solution)/shard_map/ppermute | solution.py:462
  161.7 16.6 %collective-permute-done.46.refs_23_.refs_24_ = bf16[4,80,1280]{2,1,0:T(8,128)(2,1)} collective-permute-done((bf16[4,80,1280]{2,1,0:T(8,128)(2,1)}, bf16[4,80,1280]{2,1,0:T(8,128)(2,1)}, u32[]{:S(2)}, u32[]{:S(2)}) %collective-permute-start.46) | collective-permute-done | bytes 819232 | tf_op jit(solution)/shard_map/ppermute | solution.py:462
  179.3 23.8 %attention_forward.2 = (bf16[4,512,160]{2,1,0:T(8,128)(2,1)}, f32[8,2048]{1,0:T(8,128)}) custom-call(s32[29]{0:T(128)} %concatenate.100.refs_0_, bf16[512,640]{1,0:T(8,128)(2,1)} %add_convert_fusion.14.refs_1_, bf16[512,640]{1,0:T(8,128)(2,1)} %copy-done.79, bf16[512,640]{1,0:T(8,128)(2,1)} %collective-permute-done.6.refs_3_, ...), custom_call_target="tpu_custom_call" | custom-call | flops 30799998976 | bytes 1000000 | tf_op jit(solution)/shard_map/attention_forward/pallas_call | solution.py:124
  233.5 16.8 %rows_forward.2 = (f32[512,640]{1,0:T(8,128)}, f32[512,640]{1,0:T(8,128)}, bf16[512,640]{1,0:T(8,128)(2,1)}) custom-call(s32[9]{0:T(128)} %concatenate.99.refs_0_, bf16[4,512,160]{2,1,0:T(8,128)(2,1)} %pad_maximum_fusion.5.refs_1_, f32[512,640]{1,0:T(8,128)} %convert_element_type.785.refs_2_, f32[16,640]{1,0:T(8,128)} %get-tuple-element.288.refs_3_.refs_4_, ...), custom_call_target="tpu_custom_call" | custom-call | flops 17600000000 | bytes 1000000 | tf_op jit(solution)/shard_map/rows_forward/pallas_call | solution.py:344
  267.2 14.7 %collective-permute-done.81.refs_15_.refs_16_ = bf16[4,80,1280]{2,1,0:T(8,128)(2,1)S(1)} collective-permute-done((bf16[4,80,1280]{2,1,0:T(8,128)(2,1)S(1)}, bf16[4,80,1280]{2,1,0:T(8,128)(2,1)S(1)}, u32[]{:S(2)}, u32[]{:S(2)}) %collective-permute-start.81) | collective-permute-done | bytes 819232 | tf_op jit(solution)/shard_map/ppermute | solution.py:462
  283.0 15.7 %collective-permute-done.90.refs_23_.refs_24_ = bf16[4,80,1280]{2,1,0:T(8,128)(2,1)} collective-permute-done((bf16[4,80,1280]{2,1,0:T(8,128)(2,1)S(1)}, bf16[4,80,1280]{2,1,0:T(8,128)(2,1)}, u32[]{:S(2)}, u32[]{:S(2)}) %collective-permute-start.90) | collective-permute-done | bytes 819232 | tf_op jit(solution)/shard_map/ppermute | solution.py:462
  300.4 23.3 %attention_forward.3 = (bf16[4,512,160]{2,1,0:T(8,128)(2,1)}, f32[8,2048]{1,0:T(8,128)}) custom-call(s32[29]{0:T(128)} %concatenate.100.refs_0_, bf16[512,640]{1,0:T(8,128)(2,1)} %get-tuple-element.72.refs_1_, bf16[512,640]{1,0:T(8,128)(2,1)} %copy-done.81, bf16[512,640]{1,0:T(8,128)(2,1)} %copy-done.82, bf16[512,640]{1,0:T(8,128)(2,1)} %copy-done.83, ...), custom_call_target="tpu_custom_call" | custom-call | flops 30799998976 | bytes 1000000 | tf_op jit(solution)/shard_map/attention_forward/pallas_call | solution.py:124
  345.1 16.5 %rows_forward.3 = (f32[512,640]{1,0:T(8,128)}, f32[512,640]{1,0:T(8,128)}) custom-call(s32[9]{0:T(128)} %concatenate.99.refs_0_, bf16[4,512,160]{2,1,0:T(8,128)(2,1)} %pad_maximum_fusion.6.refs_1_, f32[512,640]{1,0:T(8,128)} %get-tuple-element.74.refs_2_, f32[16,640]{1,0:T(8,128)} %get-tuple-element.287.refs_3_.refs_4_, ...), custom_call_target="tpu_custom_call" | custom-call | flops 17600000000 | bytes 1000000 | tf_op jit(solution)/shard_map/rows_forward/pallas_call | solution.py:344
  364.6 33.5 %rows_backward.2 = (f32[512,640]{1,0:T(8,128)}, bf16[4,512,160]{2,1,0:T(8,128)(2,1)}, f32[4,1,1280]{2,1,0:T(1,128)}, f32[8,640]{1,0:T(8,128)}, bf16[4,4,80,160]{...) custom-call(s32[9]{0:T(128)} %concatenate.99.refs_0_, ...), custom_call_target="tpu_custom_call" | custom-call | flops 36300001280 | bytes 1000000 | tf_op jit(solution)/shard_map/rows_backward/pallas_call | solution.py:435
  405.1 11.3 %collective-permute-start.96 = (f32[512,640]{1,0:T(8,128)}, f32[512,640]{1,0:T(8,128)}, u32[]{:S(2)}, u32[]{:S(2)}) collective-permute-start(f32[512,640]{1,0:T(8,128)} %get-tuple-element.302), channel_id=1, source_target_pairs={{0,0},{2,4},{4,2},{6,6},{1,1},{3,5},{5,3},{7,7},{8,8},{10,12},{12,... | collective-permute-start | bytes 3932168 | tf_op jit(solution)/shard_map/ppermute | solution.py:466
  420.2 48.1 %attention_backward.2 = (bf16[4,512,640]{2,1,0:T(8,128)(2,1)}, f32[2,160]{1,0:T(2,128)}, bf16[4,80,480]{2,1,0:T(8,128)(2,1)}, bf16[4,80,480]{2,1,0:T(8,128)(2,1)}) custom-call(s32[29]{0:T(128)} %concatenate.100.refs_0_, bf16[512,640]{1,0:T(8,128)(2,1)} %get-tuple-element.72.refs_1_, bf16[512,640]{1,0:T(8,128)(2,1)} %copy-done.81, ...), custom_call_target="tpu_custom_call" | custom-call | flops 60500000768 | bytes 1000000 | tf_op jit(solution)/shard_map/attention_backward/pallas_call | solution.py:242
  470.6 13.5 %collective-permute-start.123 = (bf16[2,4,80,160]{3,2,1,0:T(8,128)(2,1)S(1)}, bf16[2,4,80,160]{3,2,1,0:T(8,128)(2,1)S(1)}, u32[]{:S(2)}, u32[]{:S(2)}) collective-permute-start(bf16[2,4,80,160]{3,2,1,0:T(8,128)(2,1)S(1)} %pad_maximum_fusion.18), channel_id=1, source_target_pairs={{0,16},{16,0},{1,17},{17,1},{2,18},{18,2},{3,19},{19,3},{4,20},{20... | collective-permute-start | bytes 614408 | tf_op jit(solution)/shard_map/ppermute | solution.py:462
  517.3 12.7 %collective-permute-done.102 = bf16[512,640]{1,0:T(8,128)(2,1)S(1)} collective-permute-done((bf16[512,640]{1,0:T(8,128)(2,1)S(1)}, bf16[512,640]{1,0:T(8,128)(2,1)S(1)}, u32[]{:S(2)}, u32[]{:S(2)}) %collective-permute-start.102) | collective-permute-done | bytes 655392 | tf_op jit(solution)/shard_map/ppermute | solution.py:462
  533.0 33.6 %rows_backward.3 = (f32[512,640]{1,0:T(8,128)}, bf16[4,512,160]{2,1,0:T(8,128)(2,1)}, f32[4,1,1280]{2,1,0:T(1,128)}, f32[8,640]{1,0:T(8,128)}, bf16[4,4,80,160]{...) custom-call(s32[9]{0:T(128)} %concatenate.99.refs_0_, ...), custom_call_target="tpu_custom_call" | custom-call | flops 36300001280 | bytes 1000000 | tf_op jit(solution)/shard_map/rows_backward/pallas_call | solution.py:435
  581.2 48.1 %attention_backward.3 = (bf16[4,512,640]{2,1,0:T(8,128)(2,1)}, f32[2,160]{1,0:T(2,128)}, bf16[4,80,480]{2,1,0:T(8,128)(2,1)}, bf16[4,80,480]{2,1,0:T(8,128)(2,1)}) custom-call(s32[29]{0:T(128)} %concatenate.100.refs_0_, bf16[512,640]{1,0:T(8,128)(2,1)} %add_convert_fusion.14.refs_1_, bf16[512,640]{1,0:T(8,128)(2,1)} %copy-done.79, ...), custom_call_target="tpu_custom_call" | custom-call | flops 60500000768 | bytes 1000000 | tf_op jit(solution)/shard_map/attention_backward/pallas_call | solution.py:242
  643.3 10.2 %collective-permute-start.115 = (bf16[4,80,160]{2,1,0:T(8,128)(2,1)S(1)}, bf16[4,80,160]{2,1,0:T(8,128)(2,1)S(1)}, u32[]{:S(2)}, u32[]{:S(2)}) collective-permute-start(bf16[4,80,160]{2,1,0:T(8,128)(2,1)S(1)} %get-tuple-element.232), channel_id=1, source_target_pairs={{0,16},{16,0},{1,17},{17,1},{2,18},{18,2},{3,19},{19,3},{4,20},{20... | collective-permute-start | bytes 307208 | tf_op jit(solution)/shard_map/ppermute | solution.py:462
  691.8 11.2 %collective-permute-done.107 = bf16[512,640]{1,0:T(8,128)(2,1)S(1)} collective-permute-done((bf16[512,640]{1,0:T(8,128)(2,1)S(1)}, bf16[512,640]{1,0:T(8,128)(2,1)S(1)}, u32[]{:S(2)}, u32[]{:S(2)}) %collective-permute-start.107) | collective-permute-done | bytes 655392 | tf_op jit(solution)/shard_map/ppermute | solution.py:462
  715.7 28.3 %collective-permute-done.149 = f32[10880]{0:T(1024)S(1)} collective-permute-done((f32[10880]{0:T(1024)S(1)}, f32[10880]{0:T(1024)S(1)}, u32[]{:S(2)}, u32[]{:S(2)}) %collective-permute-start.149) | collective-permute-done | bytes 43552 | tf_op jit(solution)/shard_map/ppermute | solution.py:462
  787.9 23.9 %collective-permute-done.145 = bf16[2,80,1280]{2,1,0:T(8,128)(2,1)S(1)} collective-permute-done((bf16[2,80,1280]{2,1,0:T(8,128)(2,1)S(1)}, bf16[2,80,1280]{2,1,0:T(8,128)(2,1)S(1)}, u32[]{:S(2)}, u32[]{:S(2)}) %collective-permute-start.145) | collective-permute-done | bytes 409632 | tf_op jit(solution)/shard_map/ppermute | solution.py:462
  834.2 14.6 %collective-permute-done.134 = bf16[4,80,1280]{2,1,0:T(8,128)(2,1)S(1)} collective-permute-done((bf16[4,80,1280]{2,1,0:T(8,128)(2,1)S(1)}, bf16[4,80,1280]{2,1,0:T(8,128)(2,1)S(1)}, u32[]{:S(2)}, u32[]{:S(2)}) %collective-permute-start.134) | collective-permute-done | bytes 819232 | tf_op jit(solution)/shard_map/ppermute | solution.py:462
  852.4 24.7 %collective-permute-done.135 = bf16[2,80,1280]{2,1,0:T(8,128)(2,1)S(1)} collective-permute-done((bf16[2,80,1280]{2,1,0:T(8,128)(2,1)S(1)}, bf16[2,80,1280]{2,1,0:T(8,128)(2,1)S(1)}, u32[]{:S(2)}, u32[]{:S(2)}) %collective-permute-start.135) | collective-permute-done | bytes 409632 | tf_op jit(solution)/shard_map/ppermute | solution.py:462
  877.3 8.6 collective-permute-done.130
  (723 shorter events, 397.5 us)
Async XLA Ops:
  4.5 61.5 %collective-permute-start.1 = (bf16[512,640]{1,0:T(8,128)(2,1)}, bf16[512,640]{1,0:T(8,128)(2,1)S(1)}, u32[]{:S(2)}, u32[]{:S(2)}) collective-permute-start(bf16[512,640]{1,0:T(8,128)(2,1)} %param.21), channel_id=1, source_target_pairs={{0,0},{2,4},{4,2},{6,6},{1,1},{3,5},{5,3},{7,7},{8,8},{10,12},{12,... | collective-permute-start | bytes 1966088 | tf_op jit(solution)/shard_map/ppermute | solution.py:466
  94.6 42.8 %collective-permute-start.44 = (bf16[2,80,1280]{2,1,0:T(8,128)(2,1)S(1)}, bf16[2,80,1280]{2,1,0:T(8,128)(2,1)S(1)}, u32[]{:S(2)}, u32[]{:S(2)}) collective-permute-start(bf16[2,80,1280]{2,1,0:T(8,128)(2,1)S(1)} %pad_maximum_fusion.13), channel_id=1, source_target_pairs={{0,2},{2,0},{1,3},{3,1},{4,6},{6,4},{5,7},{7,5},{8,10},{10,8},{9,1... | collective-permute-start | bytes 1228808 | tf_op jit(solution)/shard_map/ppermute | solution.py:462
  95.5 50.9 %collective-permute-start.5 = (bf16[512,640]{1,0:T(8,128)(2,1)}, bf16[512,640]{1,0:T(8,128)(2,1)S(1)}, u32[]{:S(2)}, u32[]{:S(2)}) collective-permute-start(bf16[512,640]{1,0:T(8,128)(2,1)} %add_convert_fusion.14.refs_1_), channel_id=1, source_target_pairs={{0,1},{1,0},{2,3},{3,2},{4,5},{5,4},{6,7},{7,6},{8,9},{9,8},{10,11... | collective-permute-start | bytes 1966088 | tf_op jit(solution)/shard_map/ppermute | solution.py:462
  97.9 48.4 %collective-permute-start.79 = (bf16[2,80,1280]{2,1,0:T(8,128)(2,1)S(1)}, bf16[2,80,1280]{2,1,0:T(8,128)(2,1)}, u32[]{:S(2)}, u32[]{:S(2)}) collective-permute-start(bf16[2,80,1280]{2,1,0:T(8,128)(2,1)S(1)} %pad_maximum_fusion.14), channel_id=1, source_target_pairs={{0,2},{2,0},{1,3},{3,1},{4,6},{6,4},{5,7},{7,5},{8,10},{10,8},{9,1... | collective-permute-start | bytes 1228808 | tf_op jit(solution)/shard_map/ppermute | solution.py:462
  159.3 45.2 %collective-permute-start.45 = (bf16[4,80,1280]{2,1,0:T(8,128)(2,1)}, bf16[4,80,1280]{2,1,0:T(8,128)(2,1)}, u32[]{:S(2)}, u32[]{:S(2)}) collective-permute-start(bf16[4,80,1280]{2,1,0:T(8,128)(2,1)} %pad_maximum_fusion.8.refs_21_.refs_22_), channel_id=1, source_target_pairs={{0,8},{8,0},{1,9},{9,1},{2,10},{10,2},{3,11},{11,3},{4,12},{12,4},... | collective-permute-start | bytes 2457608 | tf_op jit(solution)/shard_map/ppermute | solution.py:462
  160.8 44.6 %collective-permute-start.48 = (bf16[4,80,1280]{2,1,0:T(8,128)(2,1)}, bf16[4,80,1280]{2,1,0:T(8,128)(2,1)}, u32[]{:S(2)}, u32[]{:S(2)}) collective-permute-start(bf16[4,80,1280]{2,1,0:T(8,128)(2,1)} %pad_maximum_fusion.8.refs_21_.refs_22_), channel_id=1, source_target_pairs={{0,4},{4,0},{1,5},{5,1},{2,6},{6,2},{3,7},{7,3},{8,12},{12,8},{9,1... | collective-permute-start | bytes 2457608 | tf_op jit(solution)/shard_map/ppermute | solution.py:462
  160.8 60.4 %collective-permute-start.38 = (bf16[4,80,1280]{2,1,0:T(8,128)(2,1)}, bf16[4,80,1280]{2,1,0:T(8,128)(2,1)}, u32[]{:S(2)}, u32[]{:S(2)}) collective-permute-start(bf16[4,80,1280]{2,1,0:T(8,128)(2,1)} %collective-permute-done.36.refs_14_.refs_15_), channel_id=1, source_target_pairs={{0,16},{16,0},{1,17},{17,1},{2,18},{18,2},{3,19},{19,3},{4,20},{20... | collective-permute-start | bytes 2457608 | tf_op jit(solution)/shard_map/ppermute | solution.py:462
  178.3 43.4 %collective-permute-start.40 = (bf16[4,80,1280]{2,1,0:T(8,128)(2,1)}, bf16[4,80,1280]{2,1,0:T(8,128)(2,1)}, u32[]{:S(2)}, u32[]{:S(2)}) collective-permute-start(bf16[4,80,1280]{2,1,0:T(8,128)(2,1)} %collective-permute-done.36.refs_14_.refs_15_), channel_id=1, source_target_pairs={{0,4},{4,0},{1,5},{5,1},{2,6},{6,2},{3,7},{7,3},{8,12},{12,8},{9,1... | collective-permute-start | bytes 2457608 | tf_op jit(solution)/shard_map/ppermute | solution.py:462
  178.3 43.4 %collective-permute-start.47 = (bf16[4,80,1280]{2,1,0:T(8,128)(2,1)}, bf16[4,80,1280]{2,1,0:T(8,128)(2,1)}, u32[]{:S(2)}, u32[]{:S(2)}) collective-permute-start(bf16[4,80,1280]{2,1,0:T(8,128)(2,1)} %collective-permute-done.46.refs_23_.refs_24_), channel_id=1, source_target_pairs={{0,8},{8,0},{1,9},{9,1},{2,10},{10,2},{3,11},{11,3},{4,12},{12,4},... | collective-permute-start | bytes 2457608 | tf_op jit(solution)/shard_map/ppermute | solution.py:462
  261.6 37.1 %collective-permute-start.90 = (bf16[4,80,1280]{2,1,0:T(8,128)(2,1)S(1)}, bf16[4,80,1280]{2,1,0:T(8,128)(2,1)}, u32[]{:S(2)}, u32[]{:S(2)}) collective-permute-start(bf16[4,80,1280]{2,1,0:T(8,128)(2,1)S(1)} %pad_maximum_fusion.10.refs_21_.refs_22_), channel_id=1, source_target_pairs={{0,16},{16,0},{1,17},{17,1},{2,18},{18,2},{3,19},{19,3},{4,20},{20... | collective-permute-start | bytes 2457608 | tf_op jit(solution)/shard_map/ppermute | solution.py:462
  281.9 43.2 %collective-permute-start.89 = (bf16[4,80,1280]{2,1,0:T(8,128)(2,1)S(1)}, bf16[4,80,1280]{2,1,0:T(8,128)(2,1)}, u32[]{:S(2)}, u32[]{:S(2)}) collective-permute-start(bf16[4,80,1280]{2,1,0:T(8,128)(2,1)S(1)} %pad_maximum_fusion.10.refs_21_.refs_22_), channel_id=1, source_target_pairs={{0,8},{8,0},{1,9},{9,1},{2,10},{10,2},{3,11},{11,3},{4,12},{12,4},... | collective-permute-start | bytes 2457608 | tf_op jit(solution)/shard_map/ppermute | solution.py:462
  283.0 43.6 %collective-permute-start.92 = (bf16[4,80,1280]{2,1,0:T(8,128)(2,1)S(1)}, bf16[4,80,1280]{2,1,0:T(8,128)(2,1)}, u32[]{:S(2)}, u32[]{:S(2)}) collective-permute-start(bf16[4,80,1280]{2,1,0:T(8,128)(2,1)S(1)} %pad_maximum_fusion.10.refs_21_.refs_22_), channel_id=1, source_target_pairs={{0,4},{4,0},{1,5},{5,1},{2,6},{6,2},{3,7},{7,3},{8,12},{12,8},{9,1... | collective-permute-start | bytes 2457608 | tf_op jit(solution)/shard_map/ppermute | solution.py:462
  405.1 112.1 %collective-permute-start.96 = (f32[512,640]{1,0:T(8,128)}, f32[512,640]{1,0:T(8,128)}, u32[]{:S(2)}, u32[]{:S(2)}) collective-permute-start(f32[512,640]{1,0:T(8,128)} %get-tuple-element.302), channel_id=1, source_target_pairs={{0,0},{2,4},{4,2},{6,6},{1,1},{3,5},{5,3},{7,7},{8,8},{10,12},{12,... | collective-permute-start | bytes 3932168 | tf_op jit(solution)/shard_map/ppermute | solution.py:466
  416.4 54.0 %collective-permute-start.122 = (bf16[4,4,80,160]{3,2,1,0:T(8,128)(2,1)S(1)}, bf16[4,4,80,160]{3,2,1,0:T(8,128)(2,1)S(1)}, u32[]{:S(2)}, u32[]{:S(2)}) collective-permute-start(bf16[4,4,80,160]{3,2,1,0:T(8,128)(2,1)S(1)} %copy-done.84), channel_id=1, source_target_pairs={{0,4},{4,0},{1,5},{5,1},{2,6},{6,2},{3,7},{7,3},{8,12},{12,8},{9,1... | collective-permute-start | bytes 1228808 | tf_op jit(solution)/shard_map/ppermute | solution.py:462
  417.1 265.9 %collective-permute-start.142 = (bf16[4,4,80,1280]{3,2,1,0:T(8,128)(2,1)}, bf16[4,4,80,1280]{3,2,1,0:T(8,128)(2,1)}, u32[]{:S(2)}, u32[]{:S(2)}) collective-permute-start(bf16[4,4,80,1280]{3,2,1,0:T(8,128)(2,1)} %get-tuple-element.101), channel_id=1, source_target_pairs={{0,4},{4,0},{1,5},{5,1},{2,6},{6,2},{3,7},{7,3},{8,12},{12,8},{9,1... | collective-permute-start | bytes 9830408 | tf_op jit(solution)/shard_map/ppermute | solution.py:462
  469.9 41.0 %collective-permute-start.101 = (bf16[2,512,640]{2,1,0:T(8,128)(2,1)S(1)}, bf16[2,512,640]{2,1,0:T(8,128)(2,1)S(1)}, u32[]{:S(2)}, u32[]{:S(2)}) collective-permute-start(bf16[2,512,640]{2,1,0:T(8,128)(2,1)S(1)} %slice.818), channel_id=1, source_target_pairs={{0,4},{4,0},{1,5},{5,1},{2,6},{6,2},{3,7},{7,3},{8,12},{12,8},{9,1... | collective-permute-start | bytes 3932168 | tf_op jit(solution)/shard_map/ppermute | solution.py:462
  498.2 189.9 %collective-permute-start.137 = (bf16[4,4,80,1280]{3,2,1,0:T(8,128)(2,1)}, bf16[4,4,80,1280]{3,2,1,0:T(8,128)(2,1)S(1)}, u32[]{:S(2)}, u32[]{:S(2)}) collective-permute-start(bf16[4,4,80,1280]{3,2,1,0:T(8,128)(2,1)} %get-tuple-element.99), channel_id=1, source_target_pairs={{0,4},{4,0},{1,5},{5,1},{2,6},{6,2},{3,7},{7,3},{8,12},{12,8},{9,1... | collective-permute-start | bytes 9830408 | tf_op jit(solution)/shard_map/ppermute | solution.py:462
  580.7 49.6 %collective-permute-start.113 = (bf16[4,4,80,160]{3,2,1,0:T(8,128)(2,1)}, bf16[4,4,80,160]{3,2,1,0:T(8,128)(2,1)}, u32[]{:S(2)}, u32[]{:S(2)}) collective-permute-start(bf16[4,4,80,160]{3,2,1,0:T(8,128)(2,1)} %get-tuple-element.89), channel_id=1, source_target_pairs={{0,4},{4,0},{1,5},{5,1},{2,6},{6,2},{3,7},{7,3},{8,12},{12,8},{9,1... | collective-permute-start | bytes 1228808 | tf_op jit(solution)/shard_map/ppermute | solution.py:462
  580.7 182.8 %collective-permute-start.132 = (bf16[4,4,80,1280]{3,2,1,0:T(8,128)(2,1)}, bf16[4,4,80,1280]{3,2,1,0:T(8,128)(2,1)}, u32[]{:S(2)}, u32[]{:S(2)}) collective-permute-start(bf16[4,4,80,1280]{3,2,1,0:T(8,128)(2,1)} %get-tuple-element.97), channel_id=1, source_target_pairs={{0,4},{4,0},{1,5},{5,1},{2,6},{6,2},{3,7},{7,3},{8,12},{12,8},{9,1... | collective-permute-start | bytes 9830408 | tf_op jit(solution)/shard_map/ppermute | solution.py:462
  657.0 110.9 %collective-permute-start.127 = (bf16[4,4,80,1280]{3,2,1,0:T(8,128)(2,1)}, bf16[4,4,80,1280]{3,2,1,0:T(8,128)(2,1)}, u32[]{:S(2)}, u32[]{:S(2)}) collective-permute-start(bf16[4,4,80,1280]{3,2,1,0:T(8,128)(2,1)} %get-tuple-element.95), channel_id=1, source_target_pairs={{0,4},{4,0},{1,5},{5,1},{2,6},{6,2},{3,7},{7,3},{8,12},{12,8},{9,1... | collective-permute-start | bytes 9830408 | tf_op jit(solution)/shard_map/ppermute | solution.py:462
  687.1 68.0 %collective-permute-start.143 = (bf16[2,4,80,1280]{3,2,1,0:T(8,128)(2,1)}, bf16[2,4,80,1280]{3,2,1,0:T(8,128)(2,1)}, u32[]{:S(2)}, u32[]{:S(2)}) collective-permute-start(bf16[2,4,80,1280]{3,2,1,0:T(8,128)(2,1)} %pad_maximum_fusion.3), channel_id=1, source_target_pairs={{0,8},{8,0},{1,9},{9,1},{2,10},{10,2},{3,11},{11,3},{4,12},{12,4},... | collective-permute-start | bytes 4915208 | tf_op jit(solution)/shard_map/ppermute | solution.py:462
  705.5 54.2 %collective-permute-start.138 = (bf16[2,4,80,1280]{3,2,1,0:T(8,128)(2,1)}, bf16[2,4,80,1280]{3,2,1,0:T(8,128)(2,1)}, u32[]{:S(2)}, u32[]{:S(2)}) collective-permute-start(bf16[2,4,80,1280]{3,2,1,0:T(8,128)(2,1)} %pad_maximum_fusion.2), channel_id=1, source_target_pairs={{0,16},{16,0},{1,17},{17,1},{2,18},{18,2},{3,19},{19,3},{4,20},{20... | collective-permute-start | bytes 4915208 | tf_op jit(solution)/shard_map/ppermute | solution.py:462
  766.7 59.9 %collective-permute-start.133 = (bf16[2,4,80,1280]{3,2,1,0:T(8,128)(2,1)S(1)}, bf16[2,4,80,1280]{3,2,1,0:T(8,128)(2,1)S(1)}, u32[]{:S(2)}, u32[]{:S(2)}) collective-permute-start(bf16[2,4,80,1280]{3,2,1,0:T(8,128)(2,1)S(1)} %pad_maximum_fusion.1), channel_id=1, source_target_pairs={{0,8},{8,0},{1,9},{9,1},{2,10},{10,2},{3,11},{11,3},{4,12},{12,4},... | collective-permute-start | bytes 4915208 | tf_op jit(solution)/shard_map/ppermute | solution.py:462
  770.4 59.9 %collective-permute-start.128 = (bf16[2,4,80,1280]{3,2,1,0:T(8,128)(2,1)S(1)}, bf16[2,4,80,1280]{3,2,1,0:T(8,128)(2,1)S(1)}, u32[]{:S(2)}, u32[]{:S(2)}) collective-permute-start(bf16[2,4,80,1280]{3,2,1,0:T(8,128)(2,1)S(1)} %pad_maximum_fusion), channel_id=1, source_target_pairs={{0,16},{16,0},{1,17},{17,1},{2,18},{18,2},{3,19},{19,3},{4,20},{20... | collective-permute-start | bytes 4915208 | tf_op jit(solution)/shard_map/ppermute | solution.py:462
  (250 other events, 3778.7 us)

commit v2 on v1

--- a/solution.py
+++ b/solution.py
@@ -28,29 +28,32 @@
     return lax.dot_general(a, b, (((1,), (1,)), ((), ())), preferred_element_type=F32)
 
 
-def load_parts(scal, parts, dest, first, rows, sem, axis):
+def load_parts(scal, parts, dest, first, rows, sem):
     copies = []
     for i, part in enumerate(parts):
         start = pl.multiple_of(scal[first + i] * rows, rows)
-        at = dest.at[pl.ds(start, rows)] if axis == 0 else dest.at[:, pl.ds(start, rows)]
-        copies.append(pltpu.make_async_copy(part, at, sem))
+        copies.append(pltpu.make_async_copy(part, dest.at[pl.ds(start, rows)], sem))
     for copy in copies:
         copy.start()
     return copies
 
 
-def attn_fwd_kernel(nb, npc, *refs):
+def chunks_of(wrefs, layer):
+    return [w.at[core, layer] for core in range(wrefs[0].shape[0]) for w in wrefs]
+
+
+def attn_fwd_kernel(nb, nw, layer, *refs):
     scal = refs[0]
     xparts = refs[1:5]
-    wparts = refs[5:5 + npc]
-    bias, segk, segq, out, lse = refs[5 + npc:10 + npc]
-    xs, ws, ks, qt, vt, acc, scores, sems = refs[10 + npc:]
+    wparts = chunks_of(refs[5:5 + nw], layer)
+    bias, segk, segq, out, lse = refs[5 + nw:10 + nw]
+    xs, ws, ks, qt, vt, acc, scores, sems = refs[10 + nw:]
     heads = ks.shape[0]
     width = heads * HEAD_DIM
     rows = xparts[0].shape[0]
     base = 2 * nb
-    wcopies = load_parts(scal, wparts, ws, base + 5, wparts[0].shape[0], sems.at[4], 0)
-    xcopies = [load_parts(scal, [p], xs, base + i, rows, sems.at[i], 0)[0] for i, p in enumerate(xparts)]
+    wcopies = load_parts(scal, wparts, ws, base + 5, wparts[0].shape[0], sems.at[4])
+    xcopies = [load_parts(scal, [p], xs, base + i, rows, sems.at[i])[0] for i, p in enumerate(xparts)]
     for c in wcopies:
         c.wait()
     for i in range(4):
@@ -112,17 +115,17 @@
     lax.fori_loop(0, nb, q_block, 0)
 
 
-def attn_fwd(scal, xparts, wparts, bias, segk, segq):
+def attn_fwd(scal, xparts, wparts, layer, bias, segk, segq):
     rows, d = xparts[0].shape
     t = 4 * rows
-    width = wparts[0].shape[1] // 3
+    width = wparts[0].shape[3] // 3
     heads = width // HEAD_DIM
     nb = t // BLK
     npc = len(wparts)
     anyspec = pl.BlockSpec(memory_space=pl.ANY)
     v = pl.BlockSpec(memory_space=pltpu.VMEM)
     return pl.pallas_call(
-        functools.partial(attn_fwd_kernel, nb, npc),
+        functools.partial(attn_fwd_kernel, nb, npc, layer),
         out_shape=(jax.ShapeDtypeStruct((4, rows, width), BF), jax.ShapeDtypeStruct((8, t), F32)),
         in_specs=[pl.BlockSpec(memory_space=pltpu.SMEM)] + [anyspec] * (4 + npc) + [v] * 3,
         out_specs=(v, v),
@@ -138,20 +141,22 @@
     )(scal, *xparts, *wparts, bias, segk, segq)
 
 
-def attn_bwd_kernel(nb, npc, groups, *refs):
+def attn_bwd_kernel(nb, nw, layer, *refs):
     scal = refs[0]
     xparts = refs[1:5]
-    wparts = refs[5:5 + npc]
-    daparts = refs[5 + npc:9 + npc]
-    a_saved, bias, segk, segq, lse, dx, dbias = refs[9 + npc:16 + npc]
-    dw_out = refs[16 + npc:16 + npc + groups]
-    xs, ws, qs, ks, vs, das, qt, kt, dat, delta, dqt, dall, dka, dva, dw, sems, osem = refs[16 + npc + groups:]
+    groups = refs[5].shape[0]
+    wparts = chunks_of(refs[5:5 + nw], layer)
+    npc = len(wparts)
+    daparts = refs[5 + nw:9 + nw]
+    a_saved, bias, segk, segq, lse, dx, dbias = refs[9 + nw:16 + nw]
+    dw_out = refs[16 + nw:16 + nw + groups]
+    xs, ws, qs, ks, vs, das, qt, kt, dat, delta, dqt, dall, dka, dva, dw, sems, osem = refs[16 + nw + groups:]
     heads = ks.shape[0]
     width = heads * HEAD_DIM
     rows = xparts[0].shape[0]
     base = 2 * nb
-    wcopies = load_parts(scal, wparts, ws, base + 5, wparts[0].shape[0], sems.at[4], 0)
-    xcopies = [load_parts(scal, [p], xs, base + i, rows, sems.at[i], 0)[0] for i, p in enumerate(xparts)]
+    wcopies = load_parts(scal, wparts, ws, base + 5, wparts[0].shape[0], sems.at[4])
+    xcopies = [load_parts(scal, [p], xs, base + i, rows, sems.at[i])[0] for i, p in enumerate(xparts)]
     for c in wcopies:
         c.wait()
     for i in range(4):
@@ -228,10 +233,11 @@
         copy.wait()
 
 
-def attn_bwd(scal, xparts, wparts, daparts, a_saved, bias, segk, segq, lse, groups):
+def attn_bwd(scal, xparts, wparts, layer, daparts, a_saved, bias, segk, segq, lse):
     rows, d = xparts[0].shape
     t = 4 * rows
-    width = wparts[0].shape[1] // 3
+    groups, _, rows_w, width = wparts[0].shape
+    width //= 3
     heads = width // HEAD_DIM
     nb = t // BLK
     npc = len(wparts)
@@ -240,11 +246,11 @@
     head_rows = pltpu.VMEM((heads, t, HEAD_DIM), BF)
     flat = pltpu.VMEM((width, t), BF)
     return pl.pallas_call(
-        functools.partial(attn_bwd_kernel, nb, npc, groups),
+        functools.partial(attn_bwd_kernel, nb, npc, layer),
         out_shape=(
             jax.ShapeDtypeStruct((4, rows, d), BF),
             jax.ShapeDtypeStruct((2, width), F32),
-        ) + (jax.ShapeDtypeStruct((npc // groups, wparts[0].shape[0], 3 * width), BF),) * groups,
+        ) + (jax.ShapeDtypeStruct((npc, rows_w, 3 * width), BF),) * groups,
         in_specs=[pl.BlockSpec(memory_space=pltpu.SMEM)] + [anyspec] * (4 + npc) + [v] * 9,
         out_specs=(v, v) + (anyspec,) * groups,
         scratch_shapes=[
@@ -279,17 +285,19 @@
     return 0.5 * (1.0 + lax.erf(u * (1.0 / math.sqrt(2.0))))
 
 
-def start_weights(scal, first, wo_parts, w1_parts, w2_parts, wo, w1, w2, sems):
-    def spans(parts):
-        rows = parts[0].shape[1]
-        return [pl.ds(pl.multiple_of(scal[first + i] * rows, rows), rows) for i in range(len(parts))]
+PAD = 256
+
+
+def start_weights(scal, parts, specs, wo, w1, w2, sems):
+    rows, units = parts[0].shape[1], w1.shape[2]
     by_block = [[] for _ in range(5)]
-    for part, at in zip(wo_parts, spans(wo_parts)):
-        by_block[0].append(pltpu.make_async_copy(part, wo.at[:, at], sems.at[0]))
-    for z in range(4):
-        for dest, parts in ((w1, w1_parts), (w2, w2_parts)):
-            for part, at in zip(parts, spans(parts)):
-                by_block[1 + z].append(pltpu.make_async_copy(part.at[z], dest.at[z, at], sems.at[1 + z]))
+    for part, (chunk, first, count) in zip(parts, specs):
+        at = pl.ds(pl.multiple_of(scal[4 + chunk] * rows, rows), rows)
+        for z in range(first, first + count):
+            src = part.at[z - first]
+            by_block[0].append(pltpu.make_async_copy(src.at[:, 2 * units:], wo.at[z, at], sems.at[0]))
+            by_block[1 + z].append(pltpu.make_async_copy(src.at[:, :units], w1.at[z, at], sems.at[1 + z]))
+            by_block[1 + z].append(pltpu.make_async_copy(src.at[:, units:2 * units], w2.at[z, at], sems.at[1 + z]))
     for copies in by_block:
         for copy in copies:
             copy.start()
@@ -301,18 +309,18 @@
         copy.wait()
 
 
-def post_fwd_kernel(npc, last, *refs):
+def post_fwd_kernel(specs, last, *refs):
     scal = refs[0]
-    a, hidden, vec, ub = refs[1:5]
-    wo_parts, w1_parts, w2_parts = refs[5:5 + npc], refs[5 + npc:5 + 2 * npc], refs[5 + 2 * npc:5 + 3 * npc]
-    rest = refs[5 + 3 * npc:]
+    a, (hidden, vec, ub) = refs[1:5], refs[5:8]
+    parts, rest = refs[8:8 + len(specs)], refs[8 + len(specs):]
     outs, (wo, w1, w2, xn2, sems) = rest[:-5], rest[-5:]
     h1, h2 = outs[:2]
-    loads = start_weights(scal, 1, wo_parts, w1_parts, w2_parts, wo, w1, w2, sems)
+    loads = start_weights(scal, parts, specs, wo, w1, w2, sems)
     wait_all(loads[0])
+    width = a[0].shape[1]
     total = hidden[...] + vec[4:5, :]
     for i in range(4):
-        total += dot_nt(a[i], wo[lax.bitwise_xor(i, scal[0])])
+        total += dot_nt(a[i][...], wo[scal[i], :, :width])
     h1[...] = total
     normal, _ = normal_rows(total)
     xn2[...] = (normal * vec[2:3, :] + vec[3:4, :]).astype(BF)
@@ -334,40 +342,42 @@
         outs[2][...] = (normal * vec[8:9, :] + vec[9:10, :]).astype(BF)
 
 
-def post_fwd(scal, a, hidden, vec, ub, wo_parts, w1_parts, w2_parts, last):
+def post_fwd(scal, a, hidden, vec, ub, parts, specs, last):
     rows, d = hidden.shape
-    npc = len(w1_parts)
-    width, units = wo_parts[0].shape[2], w1_parts[0].shape[2]
+    units = ub.shape[2]
     anyspec = pl.BlockSpec(memory_space=pl.ANY)
     v = pl.BlockSpec(memory_space=pltpu.VMEM)
     out = [jax.ShapeDtypeStruct((rows, d), F32)] * 2 + ([] if last else [jax.ShapeDtypeStruct((rows, d), BF)])
     return pl.pallas_call(
-        functools.partial(post_fwd_kernel, npc, last),
+        functools.partial(post_fwd_kernel, specs, last),
         out_shape=out,
-        in_specs=[pl.BlockSpec(memory_space=pltpu.SMEM)] + [v] * 4 + [anyspec] * (3 * npc),
+        in_specs=[pl.BlockSpec(memory_space=pltpu.SMEM)] + [v] * 7 + [anyspec] * len(parts),
         out_specs=[v] * len(out),
         scratch_shapes=[
-            pltpu.VMEM((4, d, width), BF), pltpu.VMEM((4, d, units), BF), pltpu.VMEM((4, d, units), BF),
+            pltpu.VMEM((4, d, PAD), BF), pltpu.VMEM((4, d, units), BF), pltpu.VMEM((4, d, units), BF),
             pltpu.VMEM((rows, d), BF), pltpu.SemaphoreType.DMA((5,)),
         ],
         compiler_params=pltpu.CompilerParams(vmem_limit_bytes=VMEM_LIMIT),
         cost_estimate=cost(16),
         name="rows_forward",
-    )(scal, a, hidden, vec, ub, *wo_parts, *w1_parts, *w2_parts)
-
-
-def post_bwd_kernel(npc, groups, *refs):
+    )(scal, *a, hidden, vec, ub, *parts)
+
+
+def post_bwd_kernel(specs, groups, *refs):
     scal = refs[0]
-    a, h1, gy, vec, ub = refs[1:6]
-    wo_parts, w1_parts, w2_parts = refs[6:6 + npc], refs[6 + npc:6 + 2 * npc], refs[6 + 2 * npc:6 + 3 * npc]
-    rest = refs[6 + 3 * npc:]
-    gy1, da_out, dub, dvec = rest[:4]
-    dwo_out, dw1_out, dw2_out = rest[4:4 + groups], rest[4 + groups:4 + 2 * groups], rest[4 + 2 * groups:4 + 3 * groups]
-    wo, w1, w2, dwo, dw1, dw2, xn2, df, xn2t, dft, dxn2, sems, osem = rest[4 + 3 * groups:]
-    loads = start_weights(scal, 1, wo_parts, w1_parts, w2_parts, wo, w1, w2, sems)
-    per = npc // groups
-    rows_d = w1_parts[0].shape[1]
-    spans = [pl.ds(pl.multiple_of(scal[1 + i] * rows_d, rows_d), rows_d) for i in range(npc)]
+    a, (h1, gy, vec, ub) = refs[1:5], refs[5:9]
+    parts, rest = refs[9:9 + len(specs)], refs[9 + len(specs):]
+    gy1, dub, dvec = rest[:3]
+    da_out = rest[3:7]
+    outs = rest[7:7 + len(groups)]
+    wo, w1, w2, dwo, dw1, dw2, xn2, df, xn2t, dft, dxn2, sems, osem = rest[7 + len(groups):]
+    loads = start_weights(scal, parts, specs, wo, w1, w2, sems)
+    rows_d = parts[0].shape[1]
+    width = a[0].shape[1]
+    places = []
+    for out, chunks in zip(outs, groups):
+        for i, chunk in enumerate(chunks):
+            places.append((out.at[i], pl.ds(pl.multiple_of(scal[4 + chunk] * rows_d, rows_d), rows_d)))
     normal, inverse = normal_rows(h1[...])
     xlow = (normal * vec[2:3, :] + vec[3:4, :]).astype(BF)
     xn2[...] = xlow
@@ -398,9 +408,9 @@
             return carry
 
         lax.fori_loop(0, units // SUB, step, 0)
-        for p in range(npc):
-            for src, outs in ((dw1, dw1_out), (dw2, dw2_out)):
-                stores.append(pltpu.make_async_copy(src.at[z, spans[p]], outs[p // per].at[p % per, z], osem))
+        for out, at in places:
+            for i, src in enumerate((dw1, dw2)):
+                stores.append(pltpu.make_async_copy(src.at[z, at], out.at[z, :, i * units:(i + 1) * units], osem))
                 stores[-1].start()
     wait_all(loads[0])
     upstream = dxn2[...]
@@ -411,42 +421,42 @@
     low = total.astype(BF)
     dvec[4:5, :] = jnp.sum(low.astype(F32), axis=0, keepdims=True)
     dat = low.T
+    dwo[...] = jnp.zeros_like(dwo)
     for i in range(4):
-        slot = lax.bitwise_xor(i, scal[0])
-        dwo[slot] = dot_nn(dat, a[i]).astype(BF)
-        da_out[i] = dot_nn(low, wo[slot]).astype(BF)
-    for p in range(npc):
-        stores.append(pltpu.make_async_copy(dwo.at[:, spans[p]], dwo_out[p // per].at[p % per], osem))
-        stores[-1].start()
+        slot = scal[i]
+        dwo[slot, :, :width] = dot_nn(dat, a[i][...]).astype(BF)
+        da_out[i][...] = dot_nn(low, wo[slot, :, :width]).astype(BF)
+    for out, at in places:
+        for z in range(4):
+            stores.append(pltpu.make_async_copy(dwo.at[z, at], out.at[z, :, 2 * units:], osem))
+            stores[-1].start()
     wait_all(stores)
 
 
-def post_bwd(scal, a, h1, gy, vec, ub, wo_parts, w1_parts, w2_parts, groups):
+def post_bwd(scal, a, h1, gy, vec, ub, parts, specs, groups):
     rows, d = h1.shape
-    npc = len(w1_parts)
-    per = npc // groups
-    rows_d, width, units = wo_parts[0].shape[1], wo_parts[0].shape[2], w1_parts[0].shape[2]
+    rows_d, width, units = parts[0].shape[1], a[0].shape[1], ub.shape[2]
     anyspec = pl.BlockSpec(memory_space=pl.ANY)
     v = pl.BlockSpec(memory_space=pltpu.VMEM)
-    out = [jax.ShapeDtypeStruct((rows, d), F32), jax.ShapeDtypeStruct((4, rows, width), BF),
-           jax.ShapeDtypeStruct((4, 1, units), F32), jax.ShapeDtypeStruct((8, d), F32)]
-    out += [jax.ShapeDtypeStruct((per, 4, rows_d, width), BF)] * groups
-    out += [jax.ShapeDtypeStruct((per, 4, rows_d, units), BF)] * (2 * groups)
+    out = [jax.ShapeDtypeStruct((rows, d), F32), jax.ShapeDtypeStruct((4, 1, units), F32), jax.ShapeDtypeStruct((8, d), F32)]
+    out += [jax.ShapeDtypeStruct((rows, width), BF)] * 4
+    out += [jax.ShapeDtypeStruct((len(chunks), 4, rows_d, 2 * units + PAD), BF) for chunks in groups]
+    matrix = pltpu.VMEM((4, d, units), BF)
+    thin = pltpu.VMEM((4, d, PAD), BF)
     return pl.pallas_call(
-        functools.partial(post_bwd_kernel, npc, groups),
+        functools.partial(post_bwd_kernel, specs, groups),
         out_shape=out,
-        in_specs=[pl.BlockSpec(memory_space=pltpu.SMEM)] + [v] * 5 + [anyspec] * (3 * npc),
-        out_specs=[v] * 4 + [anyspec] * (3 * groups),
+        in_specs=[pl.BlockSpec(memory_space=pltpu.SMEM)] + [v] * 8 + [anyspec] * len(parts),
+        out_specs=[v] * 7 + [anyspec] * len(groups),
         scratch_shapes=[
-            pltpu.VMEM((4, d, width), BF), pltpu.VMEM((4, d, units), BF), pltpu.VMEM((4, d, units), BF),
-            pltpu.VMEM((4, d, width), BF), pltpu.VMEM((4, d, units), BF), pltpu.VMEM((4, d, units), BF),
+            thin, matrix, matrix, thin, matrix, matrix,
             pltpu.VMEM((rows, d), BF), pltpu.VMEM((rows, d), BF), pltpu.VMEM((d, rows), BF), pltpu.VMEM((d, rows), BF),
             pltpu.VMEM((rows, d), F32), pltpu.SemaphoreType.DMA((5,)), pltpu.SemaphoreType.DMA(()),
         ],
         compiler_params=pltpu.CompilerParams(vmem_limit_bytes=VMEM_LIMIT),
         cost_estimate=cost(33),
         name="rows_backward",
-    )(scal, a, h1, gy, vec, ub, *wo_parts, *w1_parts, *w2_parts)
+    )(scal, *a, h1, gy, vec, ub, *parts)
 
 
 MOMENTUM = 0.9
@@ -474,38 +484,31 @@
     return jnp.concatenate([value, swap(value, name)], axis=0)
 
 
-def plane_parts(value, x_first):
-    across = swap(value, "x")
-    along = swap(value, "y")
-    both = swap(across, "y") if x_first else swap(along, "x")
-    return [value, across, along, both]
-
-
-def core_parts(parts):
-    return parts + [swap(part, "c") for part in parts]
-
-
 def f32(value):
     return value.astype(F32)
 
 
-def reduce_plane(terms, x_first):
-    def pick(dy, dx):
-        return sum(f32(t[2 * dy + dx]) for t in terms)
-
-    if x_first:
-        got = swap(jnp.stack([pick(0, 1), pick(1, 1)]).astype(BF), "x")
-        got2 = swap((pick(1, 0) + f32(got[1])).astype(BF), "y")
-    else:
-        got = swap(jnp.stack([pick(1, 0), pick(1, 1)]).astype(BF), "y")
-        got2 = swap((pick(0, 1) + f32(got[1])).astype(BF), "x")
-    return lambda index: pick(0, 0)[index] + f32(got[0][index]) + f32(got2[index])
-
-
-def reduce_line(take):
-    got = swap(take(slice(2, 4)).astype(BF), "h")
-    got2 = swap((take(1) + f32(got[1])).astype(BF), "b")
-    return take(0) + f32(got[0]) + f32(got2)
+def after(value, *others):
+    return lax.optimization_barrier((value,) + others)[0]
+
+
+def reduce_plane(keep, rest, for_x, for_y):
+    def pair(chunk, half):
+        return f32(keep[chunk, half]) + f32(rest[chunk, half])
+
+    whole = slice(0, 4)
+    to_x = pair(1, whole) + jnp.pad(f32(for_x), ((2, 0), (0, 0), (0, 0)))
+    to_y = pair(2, whole) + jnp.pad(f32(for_y), ((0, 2), (0, 0), (0, 0)))
+    return (lambda: pair(0, whole)), swap(to_x.astype(BF), "x"), swap(to_y.astype(BF), "y")
+
+
+def reduce_h(total):
+    return total[0] + f32(swap(total[1].astype(BF), "h"))
+
+
+def scatter(value):
+    value = lax.psum_scatter(f32(value), COLS_AXES, scatter_dimension=0, tiled=True)[0]
+    return lax.psum_scatter(value, ROWS_AXES, scatter_dimension=0, tiled=True)
 
 
 def sgd_step(weight, gradient, moment, average, step_rate):
@@ -538,6 +541,18 @@
     low_attention, low_feedforward, low_vectors, low_head, low_unit = lax.optimization_barrier(
         tuple(p.astype(BF) for p in (attention, feedforward, vectors, head_bias, unit_bias))
     )
+    head_width, units = attention.shape[3], feedforward.shape[3]
+    qkv_low = jnp.concatenate([low_attention[:, i] for i in range(3)], axis=2)
+    rows_w = attention.shape[2]
+    spare_width = units // rows_w if fast else 0
+    spare = jnp.zeros((layer_count, rows_w, PAD - head_width - spare_width), BF)
+    if fast:
+        spare = jnp.concatenate([low_unit.reshape(layer_count, rows_w, spare_width), spare], axis=2)
+    ff_low = [
+        jnp.concatenate([low_feedforward[layer, 0], low_feedforward[layer, 1],
+                         low_attention[layer, 3], spare[layer]], axis=1)
+        for layer in range(layer_count)
+    ]
 
     hidden_low = home(tokens_in)
     meta = jnp.concatenate([segments[0], jnp.sum(lengths[0])[None], bucket_map])
@@ -550,37 +565,31 @@
         for axis, place in ((0, iy), (1, ix), (2, ic)):
             v8 = jnp.where(place == 1, jnp.flip(v8, axis), v8)
         full_vectors = v8.reshape(8, layer_count * 6, -1).transpose(1, 0, 2).reshape(layer_count, 6, width_d)
-        units4 = double(double(low_unit[None], "b"), "h")
-        heads_used = jnp.where(stays, low_head, swap(low_head, "h"))
-        qkv_parts, wo_parts, up_parts, down_parts = [], [], [], []
-        for layer in range(layer_count):
-            qkv = jnp.concatenate([low_attention[layer, i] for i in range(3)], axis=1)
-            far = swap(qkv, "h")
-            mine = plane_parts(jnp.where(stays, qkv, far), True)
-            theirs = plane_parts(jnp.where(stays, far, qkv), False)
-            qkv_parts.append(mine + [swap(part, "c") for part in theirs])
-            wo_parts.append(core_parts(plane_parts(double(double(low_attention[layer, 3][None], "b"), "h"), layer % 2 == 0)))
-            up_parts.append(core_parts(plane_parts(double(double(low_feedforward[layer, 0][None], "b"), "h"), True)))
-            down_parts.append(core_parts(plane_parts(double(double(low_feedforward[layer, 1][None], "b"), "h"), False)))
+        head_pad = jnp.pad(low_head, ((0, 0), (0, 14), (0, 2 * head_width)))
+        packed = jnp.concatenate([qkv_low, head_pad], axis=1)
+        far = swap(packed, "h")
+        mine, theirs = jnp.where(stays, packed, far), jnp.where(stays, far, packed)
+        heads_used = mine[:, rows_w:rows_w + 2, :head_width]
+        both_cores = jnp.stack([mine[:, :rows_w], swap(theirs[:, :rows_w], "c")])
+        across = swap(both_cores, "x")
+        qkv_parts = [both_cores, across, swap(both_cores, "y"), swap(across, "y")]
         chunk_places = [dp_place ^ (2 * (p % 4) + p // 4) for p in range(8)]
-        switch = 2 * (ic ^ ih)
-        groups = 2
+        turned = [2 * (i % 2) + i // 2 for i in range(4)]
+        slots = jnp.stack([jnp.where(stays, turned[i], turned[i ^ 2]) for i in range(4)])
+        specs = [(0, 0, 4), (1, 0, 4), (2, 0, 4), (3, 0, 2), (3, 2, 2)]
+        specs = tuple(specs + [(chunk + 4, first, count) for chunk, first, count in specs])
+        groups = ((0, 1, 2, 3), (7,), (4, 5, 6))
     else:
         full_vectors = lax.all_gather(low_vectors, ROWS_AXES, axis=2, tiled=True)
         units4 = lax.all_gather(low_unit, COLS_AXES, axis=0)
         heads_used = lax.all_gather(low_head, COLS_AXES, axis=0)[quarter]
-        whole_attention = lax.all_gather(lax.all_gather(low_attention, ROWS_AXES, axis=2, tiled=True), COLS_AXES, axis=0)
-        whole_feedforward = lax.all_gather(lax.all_gather(low_feedforward, ROWS_AXES, axis=2, tiled=True), COLS_AXES, axis=0)
-        own = whole_attention[quarter]
-        qkv_parts = [[jnp.concatenate([own[layer, i] for i in range(3)], axis=1)] for layer in range(layer_count)]
-        wo_parts = [[whole_attention[:, layer, 3]] for layer in range(layer_count)]
-        up_parts = [[whole_feedforward[:, layer, 0]] for layer in range(layer_count)]
-        down_parts = [[whole_feedforward[:, layer, 1]] for layer in range(layer_count)]
+        qkv_parts = [lax.all_gather(lax.all_gather(qkv_low, ROWS_AXES, axis=1, tiled=True), COLS_AXES, axis=0)[quarter][None]]
+        whole_ff = [lax.all_gather(lax.all_gather(w, ROWS_AXES, axis=0, tiled=True), COLS_AXES, axis=0) for w in ff_low]
         chunk_places = [jnp.int32(0)]
-        switch = quarter
-        groups = 1
+        slots = jnp.stack([quarter ^ i for i in range(4)])
+        specs = ((0, 0, 4),)
+        groups = ((0,),)
     vec = f32(full_vectors)
-    unit_rows = f32(units4)
     head_rows = f32(heads_used)
 
     positions = jnp.arange(pack_length, dtype=jnp.int32)
@@ -591,7 +600,7 @@
     places = jnp.stack([quarter ^ rel for rel in range(4)])
     chunk_array = jnp.stack(chunk_places).astype(jnp.int32)
     scal = jnp.concatenate([first_block, end_block, places, jnp.zeros((1,), jnp.int32), chunk_array]).astype(jnp.int32)
-    scal_rows = jnp.concatenate([jnp.reshape(switch, (1,)).astype(jnp.int32), chunk_array])
+    scal_rows = jnp.concatenate([slots.astype(jnp.int32), chunk_array])
     segk, segq = own_segment[:, None], own_segment[None, :]
     live_own = (quarter * rows + jnp.arange(rows) < total_live)[:, None]
     counts_float = f32(bucket_tokens)
@@ -605,32 +614,85 @@
     normal, _ = normal_rows(hidden)
     normed = (normal * vec[0, 0] + vec[0, 1]).astype(BF)
     saved = []
+    if fast:
+        line = double(double(ff_low[0][None], "h"), "b")
+        x_part, y_part = swap(line, "x"), swap(line, "y")
     for layer in range(layer_count):
         last = layer == layer_count - 1
         over = swap(normed, "b")
         normed_parts = [normed, over, swap(normed, "c"), swap(over, "c")]
-        mixed, log_total = attn_fwd(scal, normed_parts, qkv_parts[layer], head_rows[layer], segk, segq)
-        own_mixed = jnp.stack([mixed[0], swap(mixed[1], "b"), swap(mixed[2], "c"), corner(mixed[3])])
-        unit_row = unit_rows[:, layer][:, None, :]
+        if fast:
+            if layer:
+                normed_parts, x_part, y_part = lax.optimization_barrier((normed_parts, x_part, y_part))
+            if not last:
+                ahead = after(ff_low[layer + 1][None], *normed_parts)
+                ahead_h = swap(ahead, "h")
+            own_parts = [line, x_part, y_part]
+            if layer:
+                own_parts += [swap(y_part[:2], "x"), swap(x_part[2:], "y")]
+        mixed, log_total = attn_fwd(scal, normed_parts, qkv_parts, layer, head_rows[layer], segk, segq)
+        if fast:
+            if not last:
+                mixed, ahead_h = lax.optimization_barrier((mixed, ahead_h))
+            if layer:
+                mixed, own_parts = lax.optimization_barrier((mixed, own_parts))
+            else:
+                mixed, x_part, y_part = lax.optimization_barrier((mixed, x_part, y_part))
+                own_parts = [line, x_part, y_part, swap(y_part[:2], "x"), swap(x_part[2:], "y")]
+        own_mixed = [mixed[0], swap(mixed[1], "b"), swap(mixed[2], "c"), corner(mixed[3])]
         vec16 = vec_rows(layer, 0 if last else layer + 1)
-        outs = post_fwd(scal_rows, own_mixed, hidden, vec16, unit_row, wo_parts[layer], up_parts[layer], down_parts[layer], last)
-        saved.append((hidden, normed_parts, mixed, log_total, own_mixed, outs[0], unit_row, vec16))
+        if fast:
+            at = 2 * units + head_width
+            unit_row = f32(line[:, :, at:at + spare_width].reshape(4, 1, units))
+            parts = own_parts + [swap(part, "c") for part in own_parts]
+            if not last:
+                ahead = jnp.concatenate([ahead, ahead_h])
+                ahead_b = swap(after(ahead, *own_mixed), "b")
+                own_mixed, ahead_b = lax.optimization_barrier((own_mixed, ahead_b))
+                line = jnp.concatenate([ahead, ahead_b])
+                x_part, y_part = swap(line, "x"), swap(line, "y")
+        else:
+            parts = [whole_ff[layer]]
+            unit_row = f32(units4[:, layer][:, None, :])
+        outs = post_fwd(scal_rows, own_mixed, hidden, vec16, unit_row, parts, specs, last)
+        saved.append((hidden, normed_parts, mixed, log_total, own_mixed, outs[0], unit_row, vec16, parts))
         hidden = outs[1]
         if not last:
             normed = outs[2]
-    hidden_out = home(jnp.where(live_own, hidden, 0.0))
-
-    upstream = jnp.where(live_own, f32(home(cotangent)) * pack_weight, 0.0)
-    attention_grads, feedforward_grads, vector_grads, head_grads, unit_grads = [], [], [], [], []
+    hidden_out = f32(home(jnp.where(live_own, hidden, 0.0).astype(BF)))
+    hidden_out = jnp.where(stays, jnp.where(live_own, hidden, 0.0), hidden_out)
+
+    cotangent_here = home(after(cotangent, saved[0][5]))
+    upstream = jnp.where(live_own, f32(cotangent_here) * pack_weight, 0.0)
+    qkv_grads, matrix_grads, vector_grads, head_grads, unit_grads = [], [], [], [], []
+    waiting = None
     for layer in reversed(range(layer_count)):
-        hidden, normed_parts, mixed, log_total, own_mixed, middle, unit_row, vec16 = saved[layer]
-        outs = post_bwd(scal_rows, own_mixed, middle, upstream, vec16, unit_row, wo_parts[layer], up_parts[layer], down_parts[layer], groups)
-        upstream, d_mixed, d_unit, d_vec = outs[:4]
-        d_wo, d_up, d_down = outs[4:4 + groups], outs[4 + groups:4 + 2 * groups], outs[4 + 2 * groups:4 + 3 * groups]
+        hidden, normed_parts, mixed, log_total, own_mixed, middle, unit_row, vec16, parts = saved[layer]
+        outs = post_bwd(scal_rows, own_mixed, middle, upstream, vec16, unit_row, parts, specs, groups)
+        if waiting is not None:
+            outs, beside = lax.optimization_barrier((outs, waiting[1:]))
+            own = waiting[0]() + f32(beside[0]) + f32(beside[1])
+        upstream, d_unit, d_vec = outs[:3]
+        d_mixed, terms = outs[3:7], outs[7:]
         d_parts = [d_mixed[0], swap(d_mixed[1], "b"), swap(d_mixed[2], "c"), corner(d_mixed[3])]
-        outs = attn_bwd(scal, normed_parts, qkv_parts[layer], d_parts, mixed, head_rows[layer], segk, segq, log_total, groups)
+        if fast:
+            keep, send_far, send = terms
+            far_sum = (f32(keep[3]) + f32(swap(send_far, "c")[0])).astype(BF)
+            rest = swap(after(send, *d_parts), "c")
+            for_x, for_y = swap(far_sum[2:], "y"), swap(far_sum[:2], "x")
+            if waiting is not None:
+                to_b = swap(after(own[2:].astype(BF), *d_parts), "b")
+        outs = attn_bwd(scal, normed_parts, qkv_parts, layer, d_parts, mixed, head_rows[layer], segk, segq, log_total)
+        if fast:
+            outs, rest, for_x, for_y = lax.optimization_barrier((outs, rest, for_x, for_y))
+            if waiting is not None:
+                outs, to_b = lax.optimization_barrier((outs, to_b))
+                matrix_grads.append(reduce_h(own[:2] + f32(to_b)))
+            waiting = reduce_plane(keep, rest, for_x, for_y)
+        else:
+            matrix_grads.append(scatter(terms[0][0]))
         d_rows, d_head = outs[:2]
-        d_qkv = outs[2:]
+        qkv_grads.append(outs[2:])
         got = swap(d_rows[2:4], "c")
         got2 = swap((f32(d_rows[1]) + f32(got[1])).astype(BF), "b")
         d_normed = f32(d_rows[0]) + f32(got[0]) + f32(got2)
@@ -640,50 +702,49 @@
             jnp.sum(d_normed * normal, axis=0)[None], jnp.sum(d_normed, axis=0)[None], d_vec[2:6]]))
         head_grads.append(d_head)
         unit_grads.append(d_unit[:, 0])
-        if fast:
-            up_grad, down_grad, wo_grad = (
-                reduce_line(reduce_plane([keep, swap(send, "c")], x_first))
-                for (keep, send), x_first in ((d_up, False), (d_down, True), (d_wo, layer % 2 == 0))
-            )
-            other = swap(d_qkv[1], "c")
-            near = jnp.where(stays, d_qkv[0], other)
-            far = jnp.where(stays, other, d_qkv[0])
-            take = reduce_plane([jnp.stack([near, far], axis=1)], layer % 2 == 0)
-            qkv_grad = take(0) + f32(swap(take(1).astype(BF), "h"))
-        else:
-            def scatter(value):
-                value = lax.psum_scatter(f32(value), COLS_AXES, scatter_dimension=0, tiled=True)[0]
-                return lax.psum_scatter(value, ROWS_AXES, scatter_dimension=0, tiled=True)
-
-            up_grad, down_grad, wo_grad = scatter(d_up[0][0]), scatter(d_down[0][0]), scatter(d_wo[0][0])
-            empty = jnp.zeros((4,) + d_qkv[0].shape[1:], F32)
-            qkv_grad = scatter(empty.at[quarter].set(f32(d_qkv[0][0])))
-        head_width = attention.shape[3]
-        attention_grads.append(jnp.stack([qkv_grad[:, i * head_width:(i + 1) * head_width] for i in range(3)] + [wo_grad]))
-        feedforward_grads.append(jnp.stack([up_grad, down_grad]))
-    attention_gradient = jnp.stack(attention_grads[::-1])
-    feedforward_gradient = jnp.stack(feedforward_grads[::-1])
-
     vector_sum = jnp.stack(vector_grads[::-1])
     head_sum = jnp.stack(head_grads[::-1])
     unit_sum = jnp.stack(unit_grads[::-1], axis=1)
-    v_size, u_size, e_size = vector_sum.size, unit_sum.size // 4, head_sum.size
+    v_size, u_size = vector_sum.size, unit_sum.size // 4
     if fast:
+        by_core = [jnp.stack([grads[core] for grads in qkv_grads[::-1]]) for core in range(2)]
+        other = swap(by_core[1], "c")
+        near = f32(jnp.where(stays, by_core[0], other))
+        far = jnp.where(stays, other, by_core[0])
+        both = near + f32(swap(far, "h"))
         flat_v, flat_e = vector_sum.reshape(-1), head_sum.reshape(-1)
         flat_u = unit_sum.reshape(4, -1)
-        near = jnp.where(stays, flat_e, 0.0)
-        got = swap(jnp.concatenate([flat_v, flat_u[2], flat_u[3], flat_e - near]), "h")
-        flat_v = flat_v + got[:v_size]
-        flat_e = near + got[v_size + 2 * u_size:]
-        near_u = flat_u[0] + got[v_size:v_size + u_size]
-        got2 = swap(jnp.concatenate([flat_v, flat_u[1] + got[v_size + u_size:v_size + 2 * u_size]]), "b")
-        flat = jnp.concatenate([flat_v + got2[:v_size], near_u + got2[v_size:], flat_e])
-        for name in ROWS_AXES:
-            flat = flat + swap(flat, name)
-        vector_total = flat[:v_size].reshape(vector_sum.shape)
-        unit_gradient = flat[v_size:v_size + u_size].reshape(unit_bias.shape)
-        head_gradient = flat[v_size + u_size:].reshape(head_bias.shape)
+        near_e = jnp.where(stays, flat_e, 0.0)
+        got = swap(jnp.concatenate([flat_v, flat_u[1], flat_u[3], flat_e - near_e]), "h")
+        flat = jnp.concatenate([flat_v, flat_u[0], flat_u[2], near_e]) + got
+        flat = flat + swap(flat, "c")
+        both, flat, beside = lax.optimization_barrier((both, flat, waiting[1:]))
+        own = waiting[0]() + f32(beside[0]) + f32(beside[1])
+        to_b = swap(own[2:].astype(BF), "b")
+        got = swap(both[:, 1::2].astype(BF), "x")
+        flat = flat + swap(flat, "x")
+        to_b, got, flat = lax.optimization_barrier((to_b, got, flat))
+        own = own[:2] + f32(to_b)
+        to_h = swap(own[1].astype(BF), "h")
+        got2 = swap((both[:, 2] + f32(got[:, 1])).astype(BF), "y")
+        qkv_gradient = both[:, 0] + f32(got[:, 0]) + f32(got2)
+        flat = flat + swap(flat, "y")
+        sent = swap(jnp.concatenate([flat[:v_size], flat[v_size + u_size:v_size + 2 * u_size]]), "b")
+        vector_total = (flat[:v_size] + sent[:v_size]).reshape(vector_sum.shape)
+        unit_gradient = (flat[v_size:v_size + u_size] + sent[v_size:]).reshape(unit_bias.shape)
+        flat_e = flat[v_size + 2 * u_size:]
+        head_gradient = flat_e.reshape(head_bias.shape)
+        matrix_grads.append(own[0] + f32(to_h))
     else:
+        empty = jnp.zeros((4,) + qkv_grads[0][0].shape[1:], F32)
+        qkv_gradient = jnp.stack([scatter(empty.at[quarter].set(f32(grads[0][0]))) for grads in qkv_grads[::-1]])
+    matrix_gradient = jnp.stack(matrix_grads[::-1])
+    attention_gradient = jnp.stack(
+        [qkv_gradient[:, :, i * head_width:(i + 1) * head_width] for i in range(3)]
+        + [matrix_gradient[:, :, 2 * units:2 * units + head_width]], axis=1)
+    feedforward_gradient = jnp.stack([matrix_gradient[:, :, :units], matrix_gradient[:, :, units:2 * units]], axis=1)
+
+    if not fast:
         placed = jnp.zeros((4,) + head_sum.shape, F32).at[quarter].set(head_sum)
         vector_total, unit_total, head_total = lax.psum((vector_sum, unit_sum, placed), EVERY)
         unit_gradient, head_gradient = unit_total[mp_place], head_total[mp_place]

time: 904 us -> 713 us (0.79)
  waiting for transfers between devices: 395 us -> 213 us
  starting transfers between devices: 153 us -> 122 us
  local copies, waits for them, and re-layouts: 36.5 us -> 58 us
    ppermute x144 -> x74, waiting for transfers between devices: 381 us -> 197 us  [swap(): return lax.ppermute(value, name, [(0, 1), (1, 0)])]
    ppermute x144 -> x74, starting transfers between devices: 135 us -> 110 us  [swap(): return lax.ppermute(value, name, [(0, 1), (1, 0)])]
    another operation x28 -> x6, other arithmetic: 18.6 us -> 1.47 us  [the longest x2 1.2 us: local(): matrix_gradient = jnp.stack(matrix_grads[::-1])]
    unnamed x249 -> x185, local copies, waits for them, and re-layouts: 12.2 us -> 29.2 us
    add x10 -> x12, other arithmetic: 0.13 us -> 13.6 us  [the longest x2 7.86 us: local(): own = waiting[0]() + f32(beside[0]) + f32(beside[1])]
    ppermute x4, starting transfers between devices: 14.6 us -> 5.35 us  [home(): return lax.ppermute(value, ('c', 'h'), [(0, 0), (1, 2), (2, 1), (3, 3)])]
  transfers between devices with their start and end apart: 152 -> 82, of which waited for: 60 -> 30; matrix products, arithmetic and copies ran while one was open for 9% -> 12% of each run, Pallas kernels for 23% -> 30%
where the time goes in v2:
time: 713 us; the launch traced here: 704 us
  Pallas kernels  244 us (34%)
  waiting for transfers between devices  213 us (30%)
  starting transfers between devices  122 us (17%)
  other arithmetic  62.9 us (9%)
  local copies, waits for them, and re-layouts  58 us (8%)
    ppermute x74, waiting for transfers between devices, swap(): return lax.ppermute(value, name, [(0, 1), (1, 0)])  197 us
    ppermute x74, starting transfers between devices, swap(): return lax.ppermute(value, name, [(0, 1), (1, 0)])  110 us
    pallas_call x2, Pallas kernels, attn_bwd(): pl.pallas_call(functools.partial(attn_bwd_kernel, nb, npc, layer), out_sh...  96.7 us
    pallas_call x2, Pallas kernels, post_bwd(): pl.pallas_call(functools.partial(post_bwd_kernel, specs, groups), out_sha...  67.1 us
    pallas_call x2, Pallas kernels, attn_fwd(): pl.pallas_call(functools.partial(attn_fwd_kernel, nb, npc, layer), out_sh...  46.8 us
    pallas_call x2, Pallas kernels, post_fwd(): pl.pallas_call(functools.partial(post_fwd_kernel, specs, last), out_shape...  32.9 us
    unnamed x185, local copies, waits for them, and re-layouts  29.2 us
    ppermute x4, waiting for transfers between devices, corner(): return lax.ppermute(value, ('c', 'b'), [(0, 3), (1, 2), (2, 1), (3, 0)])  16.4 us
  transfers between devices with their start and end apart: 82, of which 30 were waited for; matrix products, arithmetic and copies ran while one was open for 12% of the time, Pallas kernels for 30%

profile of v2, /device:TPU:0, one launch (start us, length us, event | category | flops | bytes accessed | tf_op | source)
XLA Modules:
  0.0 703.9 jit_solution(11752921149859257484)
XLA Ops:
  25.0 23.8 %collective-permute-done.8 = bf16[2,96,480]{2,1,0:T(8,128)(2,1)S(1)} collective-permute-done((bf16[2,96,480]{2,1,0:T(8,128)(2,1)S(1)}, bf16[2,96,480]{2,1,0:T(8,128)(2,1)S(1)}, u32[]{:S(2)}, u32[]{:S(2)}) %collective-permute-start.8) | collective-permute-done | bytes 184352 | tf_op jit(solution)/shard_map/ppermute | solution.py:472
  56.3 11.3 %collective-permute-done.5.refs_2_ = bf16[512,640]{1,0:T(8,128)(2,1)S(1)} collective-permute-done((bf16[512,640]{1,0:T(8,128)(2,1)S(1)}, bf16[512,640]{1,0:T(8,128)(2,1)S(1)}, u32[]{:S(2)}, u32[]{:S(2)}) %collective-permute-start.5) | collective-permute-done | bytes 655392 | tf_op jit(solution)/shard_map/ppermute | solution.py:472
  70.4 16.5 %collective-permute-done.15 = bf16[2,80,2816]{2,1,0:T(8,128)(2,1)S(1)} collective-permute-done((bf16[2,80,2816]{2,1,0:T(8,128)(2,1)S(1)}, bf16[2,80,2816]{2,1,0:T(8,128)(2,1)S(1)}, u32[]{:S(2)}, u32[]{:S(2)}) %collective-permute-start.15) | collective-permute-done | bytes 901152 | tf_op jit(solution)/shard_map/ppermute | solution.py:472
  93.4 23.5 %attention_forward.2 = (bf16[4,512,160]{2,1,0:T(8,128)(2,1)}, f32[8,2048]{1,0:T(8,128)}) custom-call(s32[29]{0:T(128)} %concatenate.74.refs_0_, bf16[512,640]{1,0:T(8,128)(2,1)} %copy-done.26, bf16[512,640]{1,0:T(8,128)(2,1)} %copy-done.61, bf16[512,640]{1,0:T(8,128)(2,1)} %copy-done.62, bf16[512,640]{1,0:T(8,128)(2,1)} %copy-done.63, ...), custom_call_target="tpu_custom_call" | custom-call | flops 30799998976 | bytes 1000000 | tf_op jit(solution)/shard_map/attention_forward/pallas_call | solution.py:127
  117.0 12.8 %collective-permute-done.16.refs_9_.refs_10_ = bf16[4,80,2816]{2,1,0:T(8,128)(2,1)} collective-permute-done((bf16[4,80,2816]{2,1,0:T(8,128)(2,1)S(1)}, bf16[4,80,2816]{2,1,0:T(8,128)(2,1)}, u32[]{:S(2)}, u32[]{:S(2)}) %collective-permute-start.16) | collective-permute-done | bytes 1802272 | tf_op jit(solution)/shard_map/ppermute | solution.py:472
  146.7 6.6 collective-permute-done.22.refs_11_.refs_12_
  174.0 16.8 %rows_forward.2 = (f32[512,640]{1,0:T(8,128)}, f32[512,640]{1,0:T(8,128)}, bf16[512,640]{1,0:T(8,128)(2,1)}) custom-call(s32[12]{0:T(128)} %concatenate.73.refs_0_, bf16[512,160]{1,0:T(8,128)(2,1)} %get-tuple-element.143.refs_1_, bf16[512,160]{1,0:T(8,128)(2,1)} %copy-done.70, bf16[512,160]{1,0:T(8,128)(2,1)} %copy-done.71, bf16[512,160]{1,0:T(8,128)(2,1)} %copy-done.72, ...), custom_call_target="tpu_custom_call" | custom-call | flops 17600000000 | bytes 1000000 | tf_op jit(solution)/shard_map/rows_forward/pallas_call | solution.py:351
  192.9 15.0 %collective-permute-done.29.refs_2_ = bf16[512,640]{1,0:T(8,128)(2,1)S(1)} collective-permute-done((bf16[512,640]{1,0:T(8,128)(2,1)}, bf16[512,640]{1,0:T(8,128)(2,1)S(1)}, u32[]{:S(2)}, u32[]{:S(2)}) %collective-permute-start.29) | collective-permute-done | bytes 655392 | tf_op jit(solution)/shard_map/ppermute | solution.py:472
  219.3 23.3 %attention_forward.3 = (bf16[4,512,160]{2,1,0:T(8,128)(2,1)}, f32[8,2048]{1,0:T(8,128)}) custom-call(s32[29]{0:T(128)} %concatenate.74.refs_0_, bf16[512,640]{1,0:T(8,128)(2,1)} %get-tuple-element.151.refs_1_, bf16[512,640]{1,0:T(8,128)(2,1)} %copy-done.64, bf16[512,640]{1,0:T(8,128)(2,1)} %copy-done.65, bf16[512,640]{1,0:T(8,128)(2,1)} %copy-done.66, ...), custom_call_target="tpu_custom_call" | custom-call | flops 30799998976 | bytes 1000000 | tf_op jit(solution)/shard_map/attention_forward/pallas_call | solution.py:127
  247.8 6.7 collective-permute-done.36.refs_2_
  256.4 6.4 collective-permute-done.38.refs_4_
  267.1 16.2 %rows_forward.3 = (f32[512,640]{1,0:T(8,128)}, f32[512,640]{1,0:T(8,128)}) custom-call(s32[12]{0:T(128)} %concatenate.73.refs_0_, bf16[512,160]{1,0:T(8,128)(2,1)} %get-tuple-element.384.refs_1_, bf16[512,160]{1,0:T(8,128)(2,1)} %copy-done.73, bf16[512,160]{1,0:T(8,128)(2,1)} %copy-done.74, bf16[512,160]{1,0:T(8,128)(2,1)} %copy-done.75, ...), custom_call_target="tpu_custom_call" | custom-call | flops 17600000000 | bytes 1000000 | tf_op jit(solution)/shard_map/rows_forward/pallas_call | solution.py:351
  290.2 33.5 %rows_backward.2 = (f32[512,640]{1,0:T(8,128)}, f32[4,1,1280]{2,1,0:T(1,128)}, f32[8,640]{1,0:T(8,128)}, bf16[512,160]{1,0:T(8,128)(2,1)}, bf16[512,160]{1,0:T(8...) custom-call(s32[12]{0:T(128)} %concatenate.73.refs_0_, ...), custom_call_target="tpu_custom_call" | custom-call | flops 36300001280 | bytes 1000000 | tf_op jit(solution)/shard_map/rows_backward/pallas_call | solution.py:446
  323.7 19.4 %collective-permute-start.50 = (bf16[1,4,80,2816]{3,2,1,0:T(8,128)(2,1)}, bf16[1,4,80,2816]{3,2,1,0:T(8,128)(2,1)S(1)}, u32[]{:S(2)}, u32[]{:S(2)}) collective-permute-start(bf16[1,4,80,2816]{3,2,1,0:T(8,128)(2,1)} %get-tuple-element.182), channel_id=1, source_target_pairs={{0,4},{4,0},{1,5},{5,1},{2,6},{6,2},{3,7},{7,3},{8,12},{12,8},{9,1... | collective-permute-start | bytes 5406728 | tf_op jit(solution)/shard_map/ppermute | solution.py:472
  345.3 7.2 %collective-permute-done.46.refs_10_ = bf16[512,160]{1,0:T(8,128)(2,1)S(1)} collective-permute-done((bf16[512,160]{1,0:T(8,128)(2,1)}, bf16[512,160]{1,0:T(8,128)(2,1)S(1)}, u32[]{:S(2)}, u32[]{:S(2)}) %collective-permute-start.46) | collective-permute-done | bytes 163872 | tf_op jit(solution)/shard_map/ppermute | solution.py:472
  366.1 48.3 %attention_backward.2 = (bf16[4,512,640]{2,1,0:T(8,128)(2,1)}, f32[2,160]{1,0:T(2,128)}, bf16[4,80,480]{2,1,0:T(8,128)(2,1)}, bf16[4,80,480]{2,1,0:T(8,128)(2,1)}) custom-call(s32[29]{0:T(128)} %concatenate.74.refs_0_, bf16[512,640]{1,0:T(8,128)(2,1)} %get-tuple-element.151.refs_1_, bf16[512,640]{1,0:T(8,128)(2,1)} %copy-done.64, ...), custom_call_target="tpu_custom_call" | custom-call | flops 60500000768 | bytes 1000000 | tf_op jit(solution)/shard_map/attention_backward/pallas_call | solution.py:248
  432.9 6.3 collective-permute-done.54
  442.2 33.6 %rows_backward.3 = (f32[512,640]{1,0:T(8,128)}, f32[4,1,1280]{2,1,0:T(1,128)}, f32[8,640]{1,0:T(8,128)}, bf16[512,160]{1,0:T(8,128)(2,1)}, bf16[512,160]{1,0:T(8...) custom-call(s32[12]{0:T(128)} %concatenate.73.refs_0_, ...), custom_call_target="tpu_custom_call" | custom-call | flops 36300001280 | bytes 1000000 | tf_op jit(solution)/shard_map/rows_backward/pallas_call | solution.py:446
  499.0 48.4 %attention_backward.3 = (bf16[4,512,640]{2,1,0:T(8,128)(2,1)}, f32[2,160]{1,0:T(2,128)}, bf16[4,80,480]{2,1,0:T(8,128)(2,1)}, bf16[4,80,480]{2,1,0:T(8,128)(2,1)}) custom-call(s32[29]{0:T(128)} %concatenate.74.refs_0_, bf16[512,640]{1,0:T(8,128)(2,1)} %copy-done.26, bf16[512,640]{1,0:T(8,128)(2,1)} %copy-done.61, bf16[512,640]{1,0:T(8,128)(2,1)} %copy-done.62, ...), custom_call_target="tpu_custom_call" | custom-call | flops 60500000768 | bytes 1000000 | tf_op jit(solution)/shard_map/attention_backward/pallas_call | solution.py:248
  567.9 10.5 %collective-permute-start.73 = (bf16[4,80,2816]{2,1,0:T(8,128)(2,1)}, bf16[4,80,2816]{2,1,0:T(8,128)(2,1)}, u32[]{:S(2)}, u32[]{:S(2)}) collective-permute-start(bf16[4,80,2816]{2,1,0:T(8,128)(2,1)} %get-tuple-element.368), channel_id=1, source_target_pairs={{0,16},{16,0},{1,17},{17,1},{2,18},{18,2},{3,19},{19,3},{4,20},{20... | collective-permute-start | bytes 5406728 | tf_op jit(solution)/shard_map/ppermute | solution.py:472
  578.5 28.1 %collective-permute-done.69 = bf16[2,4,80,480]{3,2,1,0:T(8,128)(2,1)} collective-permute-done((bf16[2,4,80,480]{3,2,1,0:T(8,128)(2,1)S(1)}, bf16[2,4,80,480]{3,2,1,0:T(8,128)(2,1)}, u32[]{:S(2)}, u32[]{:S(2)}) %collective-permute-start.69) | collective-permute-done | bytes 614432 | tf_op jit(solution)/shard_map/ppermute | solution.py:472
  629.7 6.6 collective-permute-done.75
  636.2 16.2 %collective-permute-done.74 = bf16[2,80,2816]{2,1,0:T(8,128)(2,1)S(1)} collective-permute-done((bf16[2,80,2816]{2,1,0:T(8,128)(2,1)S(1)}, bf16[2,80,2816]{2,1,0:T(8,128)(2,1)S(1)}, u32[]{:S(2)}, u32[]{:S(2)}) %collective-permute-start.74) | collective-permute-done | bytes 901152 | tf_op jit(solution)/shard_map/ppermute | solution.py:472
  655.6 10.4 %collective-permute-start.80 = (f32[13440]{0:T(1024)S(1)}, f32[13440]{0:T(1024)S(1)}, u32[]{:S(2)}, u32[]{:S(2)}) collective-permute-start(f32[13440]{0:T(1024)S(1)} %add.343), channel_id=1, source_target_pairs={{0,16},{16,0},{1,17},{17,1},{2,18},{18,2},{3,19},{19,3},{4,20},{20... | collective-permute-start | bytes 161288 | tf_op jit(solution)/shard_map/ppermute | solution.py:472
  (488 shorter events, 251.6 us)
Async XLA Ops:
  4.5 44.3 %collective-permute-start.1 = (bf16[512,640]{1,0:T(8,128)(2,1)}, bf16[512,640]{1,0:T(8,128)(2,1)S(1)}, u32[]{:S(2)}, u32[]{:S(2)}) collective-permute-start(bf16[512,640]{1,0:T(8,128)(2,1)} %param.21), channel_id=1, source_target_pairs={{0,0},{2,4},{4,2},{6,6},{1,1},{3,5},{5,3},{7,7},{8,8},{10,12},{12,... | collective-permute-start | bytes 1966088 | tf_op jit(solution)/shard_map/ppermute | solution.py:476
  13.1 35.6 %collective-permute-start.8 = (bf16[2,96,480]{2,1,0:T(8,128)(2,1)S(1)}, bf16[2,96,480]{2,1,0:T(8,128)(2,1)S(1)}, u32[]{:S(2)}, u32[]{:S(2)}) collective-permute-start(bf16[2,96,480]{2,1,0:T(8,128)(2,1)S(1)} %fusion.23), channel_id=1, source_target_pairs={{0,2},{2,0},{1,3},{3,1},{4,6},{6,4},{5,7},{7,5},{8,10},{10,8},{9,1... | collective-permute-start | bytes 552968 | tf_op jit(solution)/shard_map/ppermute | solution.py:472
  15.4 38.2 %collective-permute-start.14 = (bf16[1,80,2816]{2,1,0:T(8,128)(2,1)S(1)}, bf16[1,80,2816]{2,1,0:T(8,128)(2,1)S(1)}, u32[]{:S(2)}, u32[]{:S(2)}) collective-permute-start(bf16[1,80,2816]{2,1,0:T(8,128)(2,1)S(1)} %bitcast.190), channel_id=1, source_target_pairs={{0,2},{2,0},{1,3},{3,1},{4,6},{6,4},{5,7},{7,5},{8,10},{10,8},{9,1... | collective-permute-start | bytes 1351688 | tf_op jit(solution)/shard_map/ppermute | solution.py:472
  56.3 33.8 %collective-permute-start.6 = (bf16[512,640]{1,0:T(8,128)(2,1)S(1)}, bf16[512,640]{1,0:T(8,128)(2,1)S(1)}, u32[]{:S(2)}, u32[]{:S(2)}) collective-permute-start(bf16[512,640]{1,0:T(8,128)(2,1)S(1)} %add_convert_fusion.4.refs_1_), channel_id=1, source_target_pairs={{0,4},{4,0},{1,5},{5,1},{2,6},{6,2},{3,7},{7,3},{8,12},{12,8},{9,1... | collective-permute-start | bytes 1966088 | tf_op jit(solution)/shard_map/ppermute | solution.py:472
  88.2 41.6 %collective-permute-start.16 = (bf16[4,80,2816]{2,1,0:T(8,128)(2,1)S(1)}, bf16[4,80,2816]{2,1,0:T(8,128)(2,1)}, u32[]{:S(2)}, u32[]{:S(2)}) collective-permute-start(bf16[4,80,2816]{2,1,0:T(8,128)(2,1)S(1)} %pad_maximum_fusion.refs_8_.refs_9_), channel_id=1, source_target_pairs={{0,8},{8,0},{1,9},{9,1},{2,10},{10,2},{3,11},{11,3},{4,12},{12,4},... | collective-permute-start | bytes 5406728 | tf_op jit(solution)/shard_map/ppermute | solution.py:472
  90.1 41.1 %collective-permute-start.17 = (bf16[4,80,2816]{2,1,0:T(8,128)(2,1)S(1)}, bf16[4,80,2816]{2,1,0:T(8,128)(2,1)}, u32[]{:S(2)}, u32[]{:S(2)}) collective-permute-start(bf16[4,80,2816]{2,1,0:T(8,128)(2,1)S(1)} %pad_maximum_fusion.refs_8_.refs_9_), channel_id=1, source_target_pairs={{0,16},{16,0},{1,17},{17,1},{2,18},{18,2},{3,19},{19,3},{4,20},{20... | collective-permute-start | bytes 5406728 | tf_op jit(solution)/shard_map/ppermute | solution.py:472
  171.2 41.5 %collective-permute-start.32 = (bf16[4,80,2816]{2,1,0:T(8,128)(2,1)}, bf16[4,80,2816]{2,1,0:T(8,128)(2,1)}, u32[]{:S(2)}, u32[]{:S(2)}) collective-permute-start(bf16[4,80,2816]{2,1,0:T(8,128)(2,1)} %constant_dynamic-update-slice_fusion.refs_8_.refs_9_), channel_id=1, source_target_pairs={{0,8},{8,0},{1,9},{9,1},{2,10},{10,2},{3,11},{11,3},{4,12},{12,4},... | collective-permute-start | bytes 5406728 | tf_op jit(solution)/shard_map/ppermute | solution.py:472
  172.5 41.3 %collective-permute-start.33 = (bf16[4,80,2816]{2,1,0:T(8,128)(2,1)}, bf16[4,80,2816]{2,1,0:T(8,128)(2,1)}, u32[]{:S(2)}, u32[]{:S(2)}) collective-permute-start(bf16[4,80,2816]{2,1,0:T(8,128)(2,1)} %constant_dynamic-update-slice_fusion.refs_8_.refs_9_), channel_id=1, source_target_pairs={{0,16},{16,0},{1,17},{17,1},{2,18},{18,2},{3,19},{19,3},{4,20},{20... | collective-permute-start | bytes 5406728 | tf_op jit(solution)/shard_map/ppermute | solution.py:472
  323.7 33.4 %collective-permute-start.50 = (bf16[1,4,80,2816]{3,2,1,0:T(8,128)(2,1)}, bf16[1,4,80,2816]{3,2,1,0:T(8,128)(2,1)S(1)}, u32[]{:S(2)}, u32[]{:S(2)}) collective-permute-start(bf16[1,4,80,2816]{3,2,1,0:T(8,128)(2,1)} %get-tuple-element.182), channel_id=1, source_target_pairs={{0,4},{4,0},{1,5},{5,1},{2,6},{6,2},{3,7},{7,3},{8,12},{12,8},{9,1... | collective-permute-start | bytes 5406728 | tf_op jit(solution)/shard_map/ppermute | solution.py:472
  356.3 58.1 %collective-permute-start.49 = (bf16[3,4,80,2816]{3,2,1,0:T(8,128)(2,1)}, bf16[3,4,80,2816]{3,2,1,0:T(8,128)(2,1)}, u32[]{:S(2)}, u32[]{:S(2)}) collective-permute-start(bf16[3,4,80,2816]{3,2,1,0:T(8,128)(2,1)} %get-tuple-element.180), channel_id=1, source_target_pairs={{0,4},{4,0},{1,5},{5,1},{2,6},{6,2},{3,7},{7,3},{8,12},{12,8},{9,1... | collective-permute-start | bytes 16220168 | tf_op jit(solution)/shard_map/ppermute | solution.py:472
  360.4 54.0 %collective-permute-start.51 = (bf16[2,80,2816]{2,1,0:T(8,128)(2,1)}, bf16[2,80,2816]{2,1,0:T(8,128)(2,1)S(1)}, u32[]{:S(2)}, u32[]{:S(2)}) collective-permute-start(bf16[2,80,2816]{2,1,0:T(8,128)(2,1)} %get-tuple-element.379), channel_id=1, source_target_pairs={{0,16},{16,0},{1,17},{17,1},{2,18},{18,2},{3,19},{19,3},{4,20},{20... | collective-permute-start | bytes 2703368 | tf_op jit(solution)/shard_map/ppermute | solution.py:472
  366.1 48.3 %collective-permute-start.52 = (bf16[2,80,2816]{2,1,0:T(8,128)(2,1)}, bf16[2,80,2816]{2,1,0:T(8,128)(2,1)S(1)}, u32[]{:S(2)}, u32[]{:S(2)}) collective-permute-start(bf16[2,80,2816]{2,1,0:T(8,128)(2,1)} %get-tuple-element.378), channel_id=1, source_target_pairs={{0,8},{8,0},{1,9},{9,1},{2,10},{10,2},{3,11},{11,3},{4,12},{12,4},... | collective-permute-start | bytes 2703368 | tf_op jit(solution)/shard_map/ppermute | solution.py:472
  427.7 48.1 %collective-permute-start.55 = (bf16[4,80,2816]{2,1,0:T(8,128)(2,1)}, bf16[4,80,2816]{2,1,0:T(8,128)(2,1)}, u32[]{:S(2)}, u32[]{:S(2)}) collective-permute-start(bf16[4,80,2816]{2,1,0:T(8,128)(2,1)} %get-tuple-element.371), channel_id=1, source_target_pairs={{0,8},{8,0},{1,9},{9,1},{2,10},{10,2},{3,11},{11,3},{4,12},{12,4},... | collective-permute-start | bytes 5406728 | tf_op jit(solution)/shard_map/ppermute | solution.py:472
  427.7 48.1 %collective-permute-start.56 = (bf16[4,80,2816]{2,1,0:T(8,128)(2,1)}, bf16[4,80,2816]{2,1,0:T(8,128)(2,1)}, u32[]{:S(2)}, u32[]{:S(2)}) collective-permute-start(bf16[4,80,2816]{2,1,0:T(8,128)(2,1)} %get-tuple-element.370), channel_id=1, source_target_pairs={{0,16},{16,0},{1,17},{17,1},{2,18},{18,2},{3,19},{19,3},{4,20},{20... | collective-permute-start | bytes 5406728 | tf_op jit(solution)/shard_map/ppermute | solution.py:472
  490.0 57.4 %collective-permute-start.60 = (bf16[3,4,80,2816]{3,2,1,0:T(8,128)(2,1)}, bf16[3,4,80,2816]{3,2,1,0:T(8,128)(2,1)}, u32[]{:S(2)}, u32[]{:S(2)}) collective-permute-start(bf16[3,4,80,2816]{3,2,1,0:T(8,128)(2,1)} %get-tuple-element.208), channel_id=1, source_target_pairs={{0,4},{4,0},{1,5},{5,1},{2,6},{6,2},{3,7},{7,3},{8,12},{12,8},{9,1... | collective-permute-start | bytes 16220168 | tf_op jit(solution)/shard_map/ppermute | solution.py:472
  490.3 57.1 %collective-permute-start.64 = (bf16[2,80,2816]{2,1,0:T(8,128)(2,1)}, bf16[2,80,2816]{2,1,0:T(8,128)(2,1)}, u32[]{:S(2)}, u32[]{:S(2)}) collective-permute-start(bf16[2,80,2816]{2,1,0:T(8,128)(2,1)} %slice.660), channel_id=1, source_target_pairs={{0,1},{1,0},{2,3},{3,2},{4,5},{5,4},{6,7},{7,6},{8,9},{9,8},{10,11... | collective-permute-start | bytes 2703368 | tf_op jit(solution)/shard_map/ppermute | solution.py:472
  493.9 53.5 %collective-permute-start.62 = (bf16[2,80,2816]{2,1,0:T(8,128)(2,1)}, bf16[2,80,2816]{2,1,0:T(8,128)(2,1)}, u32[]{:S(2)}, u32[]{:S(2)}) collective-permute-start(bf16[2,80,2816]{2,1,0:T(8,128)(2,1)} %get-tuple-element.377), channel_id=1, source_target_pairs={{0,16},{16,0},{1,17},{17,1},{2,18},{18,2},{3,19},{19,3},{4,20},{20... | collective-permute-start | bytes 2703368 | tf_op jit(solution)/shard_map/ppermute | solution.py:472
  499.0 48.4 %collective-permute-start.63 = (bf16[2,80,2816]{2,1,0:T(8,128)(2,1)}, bf16[2,80,2816]{2,1,0:T(8,128)(2,1)}, u32[]{:S(2)}, u32[]{:S(2)}) collective-permute-start(bf16[2,80,2816]{2,1,0:T(8,128)(2,1)} %get-tuple-element.376), channel_id=1, source_target_pairs={{0,8},{8,0},{1,9},{9,1},{2,10},{10,2},{3,11},{11,3},{4,12},{12,4},... | collective-permute-start | bytes 2703368 | tf_op jit(solution)/shard_map/ppermute | solution.py:472
  552.1 72.4 %collective-permute-start.79 = (bf16[80,2816]{1,0:T(8,128)(2,1)}, bf16[80,2816]{1,0:T(8,128)(2,1)}, u32[]{:S(2)}, u32[]{:S(2)}) collective-permute-start(bf16[80,2816]{1,0:T(8,128)(2,1)} %fusion.18), channel_id=1, source_target_pairs={{0,2},{2,0},{1,3},{3,1},{4,6},{6,4},{5,7},{7,5},{8,10},{10,8},{9,1... | collective-permute-start | bytes 1351688 | tf_op jit(solution)/shard_map/ppermute | solution.py:472
  558.0 48.6 %collective-permute-start.69 = (bf16[2,4,80,480]{3,2,1,0:T(8,128)(2,1)S(1)}, bf16[2,4,80,480]{3,2,1,0:T(8,128)(2,1)}, u32[]{:S(2)}, u32[]{:S(2)}) collective-permute-start(bf16[2,4,80,480]{3,2,1,0:T(8,128)(2,1)S(1)} %broadcast_select_fusion), channel_id=1, source_target_pairs={{0,2},{2,0},{1,3},{3,1},{4,6},{6,4},{5,7},{7,5},{8,10},{10,8},{9,1... | collective-permute-start | bytes 1843208 | tf_op jit(solution)/shard_map/ppermute | solution.py:472
  562.2 45.9 %collective-permute-start.66 = (bf16[512,640]{1,0:T(8,128)(2,1)}, bf16[512,640]{1,0:T(8,128)(2,1)}, u32[]{:S(2)}, u32[]{:S(2)}) collective-permute-start(bf16[512,640]{1,0:T(8,128)(2,1)} %fusion.14), channel_id=1, source_target_pairs={{0,1},{1,0},{2,3},{3,2},{4,5},{5,4},{6,7},{7,6},{8,9},{9,8},{10,11... | collective-permute-start | bytes 1966088 | tf_op jit(solution)/shard_map/ppermute | solution.py:472
  567.8 51.9 %collective-permute-start.72 = (bf16[4,80,2816]{2,1,0:T(8,128)(2,1)}, bf16[4,80,2816]{2,1,0:T(8,128)(2,1)}, u32[]{:S(2)}, u32[]{:S(2)}) collective-permute-start(bf16[4,80,2816]{2,1,0:T(8,128)(2,1)} %get-tuple-element.369), channel_id=1, source_target_pairs={{0,8},{8,0},{1,9},{9,1},{2,10},{10,2},{3,11},{11,3},{4,12},{12,4},... | collective-permute-start | bytes 5406728 | tf_op jit(solution)/shard_map/ppermute | solution.py:472
  567.9 51.9 %collective-permute-start.73 = (bf16[4,80,2816]{2,1,0:T(8,128)(2,1)}, bf16[4,80,2816]{2,1,0:T(8,128)(2,1)}, u32[]{:S(2)}, u32[]{:S(2)}) collective-permute-start(bf16[4,80,2816]{2,1,0:T(8,128)(2,1)} %get-tuple-element.368), channel_id=1, source_target_pairs={{0,16},{16,0},{1,17},{17,1},{2,18},{18,2},{3,19},{19,3},{4,20},{20... | collective-permute-start | bytes 5406728 | tf_op jit(solution)/shard_map/ppermute | solution.py:472
  653.8 34.9 %collective-permute-start.78 = (bf16[80,2816]{1,0:T(8,128)(2,1)S(1)}, bf16[80,2816]{1,0:T(8,128)(2,1)S(1)}, u32[]{:S(2)}, u32[]{:S(2)}) collective-permute-start(bf16[80,2816]{1,0:T(8,128)(2,1)S(1)} %fusion.17), channel_id=1, source_target_pairs={{0,2},{2,0},{1,3},{3,1},{4,6},{6,4},{5,7},{7,5},{8,10},{10,8},{9,1... | collective-permute-start | bytes 1351688 | tf_op jit(solution)/shard_map/ppermute | solution.py:472
  (142 other events, 1855.9 us)
